TPU v7x, 128 devices: a whole 4x4x4 slice. The times are simulated.
128 devices in a mesh: lat: 32 (over z, y, core), lev: 4 (over x).
Axes of the slice: x: 4, y: 4, z: 4, core: 2. Of those that a mesh axis runs over, the one named last changes fastest.
Arguments:
- grid: bfloat16 [3, 1536, 32, 2816], P(None, 'lat', 'lev'), may hold values from -6 to 6
- legendre: bfloat16 [384, 769, 1280], P(('lat', 'lev')), may hold values from -6 to 6
- gauss_weights: float32 [1280], replicated, may hold values from 0.00078125 to 0.003125
- band_counts: int32 [32], replicated, may hold values from 1 to 48, 1280 in all
- pair_m: int32 [384], replicated, may hold values from 0 to 383, each once
- vert_modes: float32 [32, 32], replicated, may hold values from -1 to 1
- mode_depth: float32 [32], replicated, may hold values from 0.5 to 50
- diffusion: float32 [32], replicated, may hold values from 1 to 100
- pressure_balance_matrix: float32 [32, 32], replicated, may hold values from -1 to 1
Outputs:
- next_grid_rows: bfloat16 [3, 1536, 32, 2816], P(None, 'lat', 'lev')
Inputs may be any that keep to these rules, and one draw needn't show every extreme that they name: `band_counts`: latitudes in each band, in band order; the bands cover all 1280 latitudes and the fullest holds 48. `pair_m`: each of 0 to 383 once.
All inputs are finite; a program needn't handle non-finite values.
Results may differ from a plain program's by a relative error of at most 0.0072.
Values may be sent and summed in bfloat16 or wider, within the bound.
A program may use at most 256 MiB of HBM per device.

v0:
```python
import math

import jax
import jax.numpy as jnp
from jax import lax
from jax.sharding import PartitionSpec as P


def dft_tables(pair_m, width, points):
    upper_wave = width - 1 - pair_m
    harmonic_order_index = jnp.stack([pair_m, pair_m, upper_wave, upper_wave], axis=1).reshape(-1)
    component = jnp.arange(2 * width, dtype=jnp.int32) % 2
    phase_index = (
        harmonic_order_index[:, None] * jnp.arange(points, dtype=jnp.int32)[None, :] % points
    )
    angles = phase_index.astype(jnp.float32) * (2.0 * math.pi / points)
    trig_values = jnp.where((component == 0)[:, None], jnp.cos(angles), -jnp.sin(angles))
    factor = jnp.where(harmonic_order_index == 0, 1.0, 2.0).astype(jnp.float32)
    forward_table = (trig_values / points).astype(jnp.bfloat16)
    inverse_table = (trig_values * factor[:, None]).astype(jnp.bfloat16)
    return (forward_table, inverse_table)


def latitude_maps(band_counts, lat_cap):
    group_count = band_counts.shape[0]
    band_starts = jnp.cumsum(band_counts) - band_counts
    groups = jnp.arange(group_count, dtype=jnp.int32)
    slot_ids = jnp.arange(group_count * lat_cap, dtype=jnp.int32)
    slot_band = slot_ids // lat_cap
    offsets = slot_ids % lat_cap
    member = groups[None, :] == slot_band[:, None]
    slot_begin = jnp.sum(jnp.where(member, band_starts[None, :], 0), axis=1)
    slot_size = jnp.sum(jnp.where(member, band_counts[None, :], 0), axis=1)
    valid_slot = offsets < slot_size
    lat_of_slot = jnp.where(valid_slot, slot_begin + offsets, 0)
    return (lat_of_slot, valid_slot, band_starts)


def helmholtz(
    harmonic_model_snapshot, ratio, vert_modes, mode_depth, diffusion, pressure_balance_matrix
):
    rotation_harmonic_coeffs = harmonic_model_snapshot[..., 0, :, :]
    velocity_spread_coeffs_map = harmonic_model_snapshot[..., 1, :, :]
    thermal_harmonic_coeffs = harmonic_model_snapshot[..., 2, :, :]
    rotation_harmonic_coeffs = rotation_harmonic_coeffs / (1.0 + diffusion[:, None] * ratio * ratio)
    modes = jnp.einsum(
        "ql,...lk->...qk", vert_modes, velocity_spread_coeffs_map, precision=lax.Precision.HIGHEST
    )
    modes = modes / (1.0 + mode_depth[:, None] * ratio)
    velocity_spread_coeffs_map = jnp.einsum(
        "ql,...qk->...lk", vert_modes, modes, precision=lax.Precision.HIGHEST
    )
    thermal_harmonic_coeffs = thermal_harmonic_coeffs - jnp.einsum(
        "ja,...ax->...jx",
        pressure_balance_matrix,
        velocity_spread_coeffs_map,
        precision=lax.Precision.HIGHEST,
    )
    return jnp.stack(
        [rotation_harmonic_coeffs, velocity_spread_coeffs_map, thermal_harmonic_coeffs], axis=-3
    )


def shards(
    grid,
    legendre,
    gauss_weights,
    band_counts,
    pair_m,
    vert_modes,
    mode_depth,
    diffusion,
    pressure_balance_matrix,
):
    lat_groups = lax.axis_size("lat")
    lev_groups = lax.axis_size("lev")
    device_count = lat_groups * lev_groups
    fields, lat_cap, lev_dev, points = grid.shape
    pair_dev, row_count, lat_total = legendre.shape
    width = row_count - 1
    half_rows = width // 2 + 1
    level_total = lev_dev * lev_groups
    my_band = lax.axis_index("lat")
    owner_index = my_band * lev_groups + lax.axis_index("lev")
    lat_of_slot, valid_slot, band_starts = latitude_maps(band_counts, lat_cap)
    band_match = jnp.arange(lat_groups, dtype=jnp.int32) == my_band
    my_start = jnp.sum(jnp.where(band_match, band_starts, 0))
    my_count = jnp.sum(jnp.where(band_match, band_counts, 0))
    row_valid = jnp.arange(lat_cap, dtype=jnp.int32) < my_count
    padded_weights = jnp.concatenate([gauss_weights, jnp.zeros((lat_cap,), jnp.float32)])
    row_weights = jnp.where(
        row_valid, lax.dynamic_slice(padded_weights, (my_start,), (lat_cap,)), 0.0
    )
    forward_table, inverse_table = dft_tables(pair_m, width, points)
    coeffs = lax.dot_general(
        forward_table, grid, (((1,), (3,)), ((), ())), preferred_element_type=jnp.float32
    )
    coeffs = (coeffs * row_weights[None, None, :, None]).astype(jnp.bfloat16)
    coeffs = coeffs.reshape(device_count, pair_dev * 4, fields, lat_cap * lev_dev)
    slot_table = jnp.take(legendre, lat_of_slot, axis=2) * valid_slot.astype(jnp.bfloat16)
    slot_table = slot_table.reshape(pair_dev, row_count, lat_groups, lat_cap)
    table_head = slot_table[:, :half_rows]
    table_tail = slot_table[:, half_rows:]
    local_waves = lax.dynamic_slice(pair_m, (owner_index * pair_dev,), (pair_dev,))
    row_ids = jnp.arange(row_count, dtype=jnp.int32)
    own_rows = row_ids[None, :] < (width - local_waves)[:, None]
    degree = jnp.where(own_rows, local_waves[:, None] + row_ids[None, :], row_ids[None, :] - 1)
    ratio = (degree * (degree + 1)).astype(jnp.float32) / float(width * (width - 1))
    tail_own = own_rows[:, half_rows:]
    received = lax.all_to_all(coeffs, ("lat", "lev"), split_axis=0, concat_axis=0, tiled=True)
    field_part = received.shape[2]
    arranged = received.reshape(
        lat_groups, lev_groups, pair_dev, 2, 2, field_part, lat_cap, lev_dev
    )
    head_spec = jnp.einsum(
        "pkgs,glpcfsd->pcfldk", table_head, arranged[:, :, :, 0], preferred_element_type=jnp.float32
    )
    tail_both = jnp.einsum(
        "pkgs,glpwcfsd->pwcfldk", table_tail, arranged, preferred_element_type=jnp.float32
    )
    tail_spec = jnp.where(tail_own[:, None, None, None, None, :], tail_both[:, 0], tail_both[:, 1])
    harmonic_model_snapshot = jnp.concatenate([head_spec, tail_spec], axis=-1)
    harmonic_space_module = harmonic_model_snapshot.reshape(
        pair_dev, 2, field_part, level_total, row_count
    )
    updated = helmholtz(
        harmonic_space_module,
        ratio[:, None, None, :],
        vert_modes,
        mode_depth,
        diffusion,
        pressure_balance_matrix,
    ).astype(jnp.bfloat16)
    updated = updated.reshape(pair_dev, 2, fields, lev_groups, lev_dev, row_count)
    head_part = jnp.einsum(
        "pkgs,prfldk->glprfsd",
        table_head,
        updated[..., :half_rows],
        preferred_element_type=jnp.float32,
    )
    masks = jnp.stack([tail_own, jnp.logical_not(tail_own)], axis=1).astype(jnp.bfloat16)
    masked = updated[:, None, ..., half_rows:] * masks[:, :, None, None, None, None, :]
    tail_parts = jnp.einsum(
        "pkgs,pwrfldk->glpwrfsd", table_tail, masked, preferred_element_type=jnp.float32
    )
    synthesis = jnp.stack(
        [tail_parts[:, :, :, 0] + head_part, tail_parts[:, :, :, 1]], axis=3
    ).astype(jnp.bfloat16)
    banded = synthesis.reshape(device_count, pair_dev * 4, fields, lat_cap * lev_dev)
    received = lax.all_to_all(banded, ("lat", "lev"), split_axis=0, concat_axis=0, tiled=True)
    field_part = received.shape[2]
    columns = received.reshape(2 * width, field_part, lat_cap * lev_dev)
    values = lax.dot_general(
        columns, inverse_table, (((0,), (0,)), ((), ())), preferred_element_type=jnp.float32
    )
    return values.reshape(field_part, lat_cap, lev_dev, points).astype(jnp.bfloat16)


def solution(mesh):
    placed = (
        P(None, "lat", "lev", None),
        P(("lat", "lev"), None, None),
        P(),
        P(),
        P(),
        P(),
        P(),
        P(),
        P(),
    )
    return jax.shard_map(
        shards, mesh=mesh, in_specs=placed, out_specs=P(None, "lat", "lev", None), check_vma=False
    )
```

profile of v0, /device:TPU:1, one launch (start us, length us, event | category | flops | bytes accessed | tf_op | source)
XLA Modules:
  0.0 694.8 jit_solution(11511353529314028400)
XLA Ops:
  6.4 74.7 %fusion.104 = bf16[1536,2816,1,1]{1,0,3,2:T(8,128)(2,1)S(1)} fusion(s32[1536]{0:T(1024)S(1)} %mul.117, pred[1536]{0:T(1024)(128)(4,1)S(1)} %fusion.75), kind=kLoop, calls=%fused_computation.18.clone.clone.clone.clone.1 | loop fusion | flops 56229888 | bytes 8658432 | tf_op jit(solution)/shard_map/dot_general | solution.py:95
  81.8 12.3 %multiply_convert_fusion.2 = bf16[1536,3,48,8]{0,2,3,1:T(8,128)(2,1)S(1)} fusion(bf16[3,48,8,2816]{3,2,1,0:T(8,128)(2,1)} %param.9, f32[48]{0:T(128)S(1)} %compare_select_fusion.4, bf16[1536,2816,1,1]{1,0,3,2:T(8,128)(2,1)S(1)} %fusion.104), kind=kOutput, calls=%fused_computation.36 | convolution fusion | flops 9969205248 | bytes 18677952 | tf_op jit(solution)/shard_map/dot_general | solution.py:95
  96.1 86.3 %reshape.253 = bf16[128,12,3,384]{1,0,3,2:T(8,128)(2,1)} reshape(bf16[1536,3,48,8]{0,3,2,1:T(8,128)(2,1)S(1)} %copy.136) | data formatting | bytes 7077888 | tf_op jit(solution)/shard_map/reshape | solution.py:99
  182.4 47.6 %copy.137 = bf16[128,12,3,384]{3,1,2,0:T(8,128)(2,1)} copy(bf16[128,12,3,384]{1,0,3,2:T(8,128)(2,1)} %reshape.253) | data formatting | bytes 7077888 | tf_op jit(solution)/shard_map/reshape | solution.py:99
  230.0 12.5 %all-to-all-start = ((bf16[128,12,3,384]{3,1,2,0:T(8,128)(2,1)}), bf16[128,12,3,384]{3,1,2,0:T(8,128)(2,1)}, u32[]{:S(2)}, u32[]{:S(2)}) async-start(bf16[128,12,3,384]{3,1,2,0:T(8,128)(2,1)} %copy.137), calls=%async_computation | async-start | bytes 9437184 | tf_op jit(solution)/shard_map/all_to_all | solution.py:110
  242.8 17.5 %copy.140 = bf16[3,769,1280]{1,0,2:T(4,128)(2,1)} copy(bf16[3,769,1280]{2,1,0:T(8,128)(2,1)} %param.10) | data formatting | bytes 11811840 | tf_op args[1]
  260.4 16.8 %gather_fusion = bf16[1536,3,769]{2,1,0:T(4,128)(2,1)} fusion(bf16[3,769,1280]{1,0,2:T(4,128)(2,1)} %copy.140, s32[2048]{0:T(1024)S(1)} %pad_clamp_fusion), kind=kCustom, calls=%fused_computation | custom fusion | bytes 14180352 | tf_op jit(solution)/shard_map/jit(_take)/gather | solution.py:100
  277.2 8.5 %copy.141 = bf16[3,769,1536]{1,2,0:T(8,128)(2,1)} copy(bf16[3,769,1536]{1,0,2:T(4,128)(2,1)} %bitcast.171) | data formatting | bytes 14174208 | tf_op jit(solution)/shard_map/jit(_take)/gather | solution.py:100
  289.0 7.5 %select_multiply_fusion = bf16[3,769,32,48]{1,3,2,0:T(8,128)(2,1)} fusion(bf16[3,769,32,48]{1,3,2,0:T(8,128)(2,1)} %bitcast.170, pred[32,48]{1,0:T(8,128)(4,1)S(1)} %compare_and_fusion, bf16[32,48]{1,0:T(8,128)(2,1)S(1)} %get-tuple-element.11), kind=kLoop, calls=%fused_computation.35 | loop fusion | flops 7087104 | bytes 14178816 | tf_op jit(solution)/shard_map/mul | solution.py:100
  296.5 4.6 all-to-all-done
  304.4 66.8 %reshape.254 = bf16[32,4,3,2,2,3,48,8]{7,6,1,0,5,4,3,2:T(8,128)(2,1)} reshape(bf16[128,12,3,384]{3,0,2,1:T(8,128)(2,1)S(1)} %copy.138) | data formatting | bytes 7077888 | tf_op jit(solution)/shard_map/reshape | solution.py:112
  371.2 19.5 %slice.55 = bf16[32,4,3,1,2,3,48,8]{7,6,1,0,5,4,3,2:T(8,128)(2,1)} slice(bf16[32,4,3,2,2,3,48,8]{7,6,1,0,5,4,3,2:T(8,128)(2,1)} %reshape.254), slice={[0:32], [0:4], [0:3], [0:1], [0:2], [0:3], [0:48], [0:8]} | slice | bytes 3538944 | tf_op jit(solution)/shard_map/slice | solution.py:116
  390.7 27.1 %fusion.44 = f32[3,2,2,3,4,8,384]{6,5,3,2,4,0,1:T(8,128)S(1)} fusion(bf16[3,769,32,48]{1,3,2,0:T(8,128)(2,1)} %select_multiply_fusion, bf16[32,4,3,2,2,3,48,8]{7,6,1,0,5,4,3,2:T(8,128)(2,1)} %reshape.254), kind=kOutput, calls=%fused_computation.51 | convolution fusion | flops 1358954496 | bytes 61931520 | tf_op jit(solution)/shard_map/pkgs,glpwcfsd->pwcfldk/dot_general | solution.py:118
  417.8 22.2 %copy.177 = bf16[32,4,3,1,2,3,48,8]{6,7,0,5,4,1,2,3:T(8,128)(2,1)} copy(bf16[32,4,3,1,2,3,48,8]{7,6,1,0,5,4,3,2:T(8,128)(2,1)} %slice.55) | data formatting | bytes 3538944
  440.0 5.2 fusion.49
  448.4 7.1 %convolution_bitcast_fusion = f32[32,4,3,2,2,3,48,8]{6,7,0,1,5,4,3,2:T(8,128)S(1)} fusion(bf16[3,769,32,48]{1,3,2,0:T(8,128)(2,1)} %select_multiply_fusion, bf16[3,2,384]{2,1,0:T(2,128)(2,1)S(1)} %copy-done.3, bf16[3,2,3,4,8,384]{5,4,3,2,1,0:T(8,128)(2,1)S(1)} %pad_maximum_fusion.5), kind=kOutput, calls=%fused_computation.34 | convolution fusion | flops 1360723968 | bytes 11063808 | tf_op jit(solution)/shard_map/pkgs,pwrfldk->glpwrfsd/dot_general | solution.py:143
  455.5 9.7 %fusion.31 = bf16[32,4,3,1,2,3,48,8]{6,7,0,1,5,4,3,2:T(8,128)(2,1)} fusion(f32[32,4,3,2,2,3,48,8]{6,7,0,1,5,4,3,2:T(8,128)S(1)} %convolution_bitcast_fusion, bf16[3,769,32,48]{1,3,2,0:T(8,128)(2,1)} %select_multiply_fusion, bf16[3,2,1,4,8,769]{5,4,3,2,1,0:T(8,128)(2,1)S(1)} %fusion.55, bf16[3,2,1,4,8,769]{5,4,3,2,1,0:T(8,128)(2,1)S(1)} %convert_bitcast_fusion, ...), kind=kOutput, calls=%fused_computation.39 | convolution fusion | flops 684346752 | bytes 10912896 | tf_op jit(solution)/shard_map/pkgs,prfldk->glprfsd/dot_general | solution.py:135
  468.4 9.5 %pad_maximum_fusion = bf16[32,4,3,2,2,3,48,8]{6,7,0,1,5,4,3,2:T(8,128)(2,1)} fusion(bf16[32,4,3,1,2,3,48,8]{6,7,0,1,5,4,3,2:T(8,128)(2,1)} %slice.109, bf16[32,4,3,1,2,3,48,8]{6,7,0,1,5,4,3,2:T(8,128)(2,1)} %fusion.31), kind=kLoop, calls=%fused_computation.17 | loop fusion | flops 1769472 | bytes 7077888 | tf_op jit(solution)/shard_map/stack | solution.py:146
  477.8 40.7 %copy.173 = bf16[32,4,3,2,2,3,48,8]{7,6,5,4,3,2,1,0:T(8,128)(2,1)} copy(bf16[32,4,3,2,2,3,48,8]{6,7,0,1,5,4,3,2:T(8,128)(2,1)} %pad_maximum_fusion) | data formatting | bytes 7077888 | tf_op jit(solution)/shard_map/convert_element_type | solution.py:148
  518.6 72.3 %reshape.276 = bf16[128,12,3,384]{3,2,1,0:T(4,128)(2,1)} reshape(bf16[32,4,3,2,2,3,48,8]{7,6,5,4,3,2,1,0:T(8,128)(2,1)} %copy.173) | data formatting | bytes 7077888 | tf_op jit(solution)/shard_map/convert_element_type | solution.py:148
  590.9 5.5 all-to-all-start.1
  596.5 76.2 %fusion.106 = bf16[1536,2816,1,1]{1,0,3,2:T(8,128)(2,1)} fusion(f32[1536]{0:T(1024)S(1)} %compare_select_fusion.3, s32[1536]{0:T(1024)S(1)} %copy-done.5, pred[1536]{0:T(1024)(128)(4,1)S(1)} %copy-done.11), kind=kLoop, calls=%fused_computation.19.clone.clone.clone.clone.1 | loop fusion | flops 56229888 | bytes 8664576 | tf_op jit(solution)/shard_map/dot_general | solution.py:153
  672.7 6.5 copy.175
  679.2 15.4 %fusion.28 = bf16[3,48,8,2816]{3,2,1,0:T(8,128)(2,1)} fusion(bf16[1536,3,384]{0,2,1:T(8,128)(2,1)S(1)} %copy.175, bf16[1536,2816,1,1]{1,0,3,2:T(8,128)(2,1)} %fusion.106), kind=kOutput, calls=%fused_computation.38 | convolution fusion | flops 9968910336 | bytes 18677760 | tf_op jit(solution)/shard_map/dot_general | solution.py:153
  (72 shorter events, 19.9 us)
Async XLA Ops:
  0.0 445.8 %copy-start = (f32[32,32]{1,0:T(8,128)S(1)}, f32[32,32]{1,0:T(8,128)}, u32[]{:S(2)}) copy-start(f32[32,32]{1,0:T(8,128)} %param.14) | copy-start | bytes 12292
  1.4 79.7 %copy-start.10 = (pred[1536]{0:T(1024)(128)(4,1)}, pred[1536]{0:T(1024)(128)(4,1)S(1)}, u32[]{:S(2)}) copy-start(pred[1536]{0:T(1024)(128)(4,1)S(1)} %fusion.75) | copy-start | bytes 4612
  5.6 75.5 %copy-start.7 = (f32[1280]{0:T(1024)S(1)}, f32[1280]{0:T(1024)}, u32[]{:S(2)}) copy-start(f32[1280]{0:T(1024)} %param.11) | copy-start | bytes 15364
  5.7 76.1 %copy-start.4 = (s32[1536]{0:T(1024)}, s32[1536]{0:T(1024)S(1)}, u32[]{:S(2)}) copy-start(s32[1536]{0:T(1024)S(1)} %mul.117) | copy-start | bytes 18436
  230.0 12.6 %copy-start.9 = (s32[32]{0:T(128)S(1)}, s32[32]{0:T(128)}, u32[]{:S(2)}) copy-start(s32[32]{0:T(128)} %param.12) | copy-start | bytes 388
  230.0 12.6 %copy-start.12 = (s32[32]{0:T(128)S(1)}, s32[32]{0:T(128)}, u32[]{:S(2)}) copy-start(s32[32]{0:T(128)} %get-tuple-element.8) | copy-start | bytes 388
  230.0 71.2 %all-to-all-start = ((bf16[128,12,3,384]{3,1,2,0:T(8,128)(2,1)}), bf16[128,12,3,384]{3,1,2,0:T(8,128)(2,1)}, u32[]{:S(2)}, u32[]{:S(2)}) async-start(bf16[128,12,3,384]{3,1,2,0:T(8,128)(2,1)} %copy.137), calls=%async_computation | async-start | bytes 9437184 | tf_op jit(solution)/shard_map/all_to_all | solution.py:110
  277.2 10.8 %copy-start.13 = (f32[32]{0:T(128)S(1)}, f32[32]{0:T(128)}, u32[]{:S(2)}) copy-start(f32[32]{0:T(128)} %param.16) | copy-start | bytes 388
  277.2 10.8 %copy-start.14 = (f32[32]{0:T(128)S(1)}, f32[32]{0:T(128)}, u32[]{:S(2)}) copy-start(f32[32]{0:T(128)} %param.15) | copy-start | bytes 388
  440.0 5.3 copy-start.8
  440.0 5.8 copy-start.2
  445.2 2.1 copy-start.6
  445.2 2.8 copy-start.1
  445.2 3.1 copy-start.3
  590.9 5.5 copy-start.5
  590.9 5.6 copy-start.11
  590.9 81.8 %all-to-all-start.1 = ((bf16[128,12,3,384]{3,2,1,0:T(4,128)(2,1)}), bf16[128,12,3,384]{3,2,1,0:T(4,128)(2,1)}, u32[]{:S(2)}, u32[]{:S(2)}) async-start(bf16[128,12,3,384]{3,2,1,0:T(4,128)(2,1)} %reshape.276), calls=%async_computation.1 | async-start | bytes 9437184 | tf_op jit(solution)/shard_map/all_to_all | solution.py:150
where the time goes:
time: 709 us; the launch traced here: 695 us
  local copies, waits for them, and re-layouts  415 us (59%)
  other arithmetic  176 us (25%)
  matrix products  79.1 us (11%)
  starting transfers between devices  18.1 us (3%)
    reshape x2, local copies, waits for them, and re-layouts, shards(): coeffs.reshape(device_count, pair_dev * 4, fields, lat_cap * lev_dev)  134 us
    convert_element_type x2, local copies, waits for them, and re-layouts, shards(): synthesis = jnp.stack([tail_parts[:, :, :, 0] + head_part, tail_parts[:,...  113 us
    dot_general x1, other arithmetic, shards(): lax.dot_general(columns, inverse_table, (((0,), (0,)), ((), ())), preferr...  76.2 us
    dot_general x1, other arithmetic, shards(): lax.dot_general(forward_table, grid, (((1,), (3,)), ((), ())), preferred_...  74.7 us
    reshape x1, local copies, waits for them, and re-layouts, shards(): received.reshape(lat_groups, lev_groups, pair_dev, 2, 2, field_part, lat_...  66.8 us
    unnamed x32, local copies, waits for them, and re-layouts  39.7 us
    dot_general x1, matrix products, shards(): jnp.einsum('pkgs,glpwcfsd->pwcfldk', table_tail, arranged, preferred_elem...  27.1 us
    gather x2, local copies, waits for them, and re-layouts, shards(): jnp.take(legendre, lat_of_slot, axis=2) * valid_slot.astype(jnp.bfloat16)  25.4 us
  transfers between devices with their start and end apart: 2, of which 1 were waited for; matrix products, arithmetic and copies ran while one was open for 19% of the time, Pallas kernels for 0%

commit v1 on v0

--- a/solution.py
+++ b/solution.py
@@ -3,6 +3,8 @@
 import jax
 import jax.numpy as jnp
 from jax import lax
+from jax.experimental import pallas as pl
+from jax.experimental.pallas import tpu as pltpu
 from jax.sharding import PartitionSpec as P
 
 
@@ -59,6 +61,69 @@
     return jnp.stack(
         [rotation_harmonic_coeffs, velocity_spread_coeffs_map, thermal_harmonic_coeffs], axis=-3
     )
+
+
+def exchange_kernel(x, o, send, recv, local):
+    lat, lev = lax.axis_index("lat"), lax.axis_index("lev")
+    me = lat * 4 + lev
+    barrier = pltpu.get_barrier_semaphore()
+
+    def greet(k, carry):
+        there = lax.rem(me + k, 128)
+        pl.semaphore_signal(
+            barrier,
+            inc=1,
+            device_id=(there // 4, lax.rem(there, 4)),
+            device_id_type=pl.DeviceIdType.MESH,
+        )
+        return carry
+
+    lax.fori_loop(1, 128, greet, 0)
+    pl.semaphore_wait(barrier, 127)
+    own = pltpu.make_async_copy(x.at[me], o.at[me], local)
+    own.start()
+
+    def launch(k, carry):
+        step = lax.rem(k * 37, 128)
+        z = lax.rem(lat // 8 + step // 32, 4)
+        y = lax.rem(lat // 2 + step // 8, 4)
+        core = lax.rem(lat + step, 2)
+        to_lat, to_lev = (z * 4 + y) * 2 + core, lax.rem(lev + step // 2, 4)
+        pltpu.make_async_remote_copy(
+            src_ref=x.at[to_lat * 4 + to_lev],
+            dst_ref=o.at[me],
+            send_sem=send,
+            recv_sem=recv,
+            device_id=(to_lat, to_lev),
+            device_id_type=pl.DeviceIdType.MESH,
+        ).start()
+        return carry
+
+    lax.fori_loop(1, 128, launch, 0)
+    own.wait()
+    rest = pltpu.make_async_remote_copy(
+        src_ref=x.at[pl.ds(0, 127)],
+        dst_ref=o.at[pl.ds(0, 127)],
+        send_sem=send,
+        recv_sem=recv,
+        device_id=(lat, lev),
+        device_id_type=pl.DeviceIdType.MESH,
+    )
+    rest.wait_send()
+    rest.wait_recv()
+
+
+def exchange(x, number):
+    shape = x.shape
+    x = x.reshape(shape[0], -1, 128)
+    return pl.pallas_call(
+        exchange_kernel,
+        out_shape=jax.ShapeDtypeStruct(x.shape, x.dtype),
+        in_specs=[pl.BlockSpec(memory_space=pl.ANY)],
+        out_specs=pl.BlockSpec(memory_space=pl.ANY),
+        scratch_shapes=[pltpu.SemaphoreType.DMA] * 3,
+        compiler_params=pltpu.CompilerParams(collective_id=number, has_side_effects=True),
+    )(x).reshape(shape)
 
 
 def shards(
@@ -107,7 +172,7 @@
     degree = jnp.where(own_rows, local_waves[:, None] + row_ids[None, :], row_ids[None, :] - 1)
     ratio = (degree * (degree + 1)).astype(jnp.float32) / float(width * (width - 1))
     tail_own = own_rows[:, half_rows:]
-    received = lax.all_to_all(coeffs, ("lat", "lev"), split_axis=0, concat_axis=0, tiled=True)
+    received = exchange(coeffs, 0)
     field_part = received.shape[2]
     arranged = received.reshape(
         lat_groups, lev_groups, pair_dev, 2, 2, field_part, lat_cap, lev_dev
@@ -147,7 +212,7 @@
         [tail_parts[:, :, :, 0] + head_part, tail_parts[:, :, :, 1]], axis=3
     ).astype(jnp.bfloat16)
     banded = synthesis.reshape(device_count, pair_dev * 4, fields, lat_cap * lev_dev)
-    received = lax.all_to_all(banded, ("lat", "lev"), split_axis=0, concat_axis=0, tiled=True)
+    received = exchange(banded, 1)
     field_part = received.shape[2]
     columns = received.reshape(2 * width, field_part, lat_cap * lev_dev)
     values = lax.dot_general(

time: 709 us -> 768 us (1.083)
  Pallas kernels: 0 us -> 105 us
  starting transfers between devices: 18.1 us -> 0 us
  local copies, waits for them, and re-layouts: 415 us -> 401 us
    reshape x3 -> x0, local copies, waits for them, and re-layouts: 201 us -> none  [the longest x2 134 us: shards(): coeffs.reshape(device_count, pair_dev * 4, fields, lat_cap * lev_dev)]
    another operation x1 -> x5, local copies, waits for them, and re-layouts: 0.74 us -> 187 us  [the longest x1 70.7 us: shards(): received.reshape(lat_groups, lev_groups, pair_dev, 2, 2, field_part, lat_...]
    pallas_call x0 -> x2, Pallas kernels: none -> 105 us  [exchange(): pl.pallas_call(exchange_kernel, out_shape=jax.ShapeDtypeStruct(x.shape, x...]
    convert_element_type x1, local copies, waits for them, and re-layouts: 1.94 us -> 54.5 us  [shards(): coeffs = (coeffs * row_weights[None, None, :, None]).astype(jnp.bfloat16)]
    convert_element_type x2 -> x1, local copies, waits for them, and re-layouts: 113 us -> 64.5 us  [shards(): synthesis = jnp.stack([tail_parts[:, :, :, 0] + head_part, tail_parts[:,...]
    all_to_all x2 -> x0, starting transfers between devices: 18.1 us -> none  [the longest x1 12.5 us: shards(): lax.all_to_all(coeffs, ('lat', 'lev'), split_axis=0, concat_axis=0, tiled...]
    unnamed x32 -> x24, local copies, waits for them, and re-layouts: 39.7 us -> 40.6 us
  transfers between devices with their start and end apart: 2 -> 0, of which waited for: 1 -> 0; matrix products, arithmetic and copies ran while one was open for 19% -> 0% of each run, Pallas kernels for 0% -> 0%
where the time goes in v1:
time: 768 us; the launch traced here: 758 us
  local copies, waits for them, and re-layouts  401 us (52%)
  other arithmetic  175 us (23%)
  Pallas kernels  105 us (14%)
  matrix products  74.8 us (10%)
    pallas_call x2, Pallas kernels, exchange(): pl.pallas_call(exchange_kernel, out_shape=jax.ShapeDtypeStruct(x.shape, x...  105 us
    dot_general x1, other arithmetic, shards(): lax.dot_general(columns, inverse_table, (((0,), (0,)), ((), ())), preferr...  76.5 us
    dot_general x1, other arithmetic, shards(): lax.dot_general(forward_table, grid, (((1,), (3,)), ((), ())), preferred_...  74.6 us
    another operation x1, local copies, waits for them, and re-layouts, shards(): received.reshape(lat_groups, lev_groups, pair_dev, 2, 2, field_part, lat_...  70.7 us
    convert_element_type x1, local copies, waits for them, and re-layouts, shards(): synthesis = jnp.stack([tail_parts[:, :, :, 0] + head_part, tail_parts[:,...  64.5 us
    another operation x1, local copies, waits for them, and re-layouts, exchange(): x = x.reshape(shape[0], -1, 128)  64.5 us
    convert_element_type x1, local copies, waits for them, and re-layouts, shards(): coeffs = (coeffs * row_weights[None, None, :, None]).astype(jnp.bfloat16)  54.5 us
    another operation x1, local copies, waits for them, and re-layouts, shards(): jnp.stack([tail_parts[:, :, :, 0] + head_part, tail_parts[:, :, :, 1]], a...  40.8 us

profile of v1, /device:TPU:1, one launch (start us, length us, event | category | flops | bytes accessed | tf_op | source)
XLA Modules:
  0.0 757.7 jit_solution(15055383332284190923)
XLA Ops:
  3.4 17.5 %copy.128 = bf16[3,769,1280]{1,0,2:T(4,128)(2,1)} copy(bf16[3,769,1280]{2,1,0:T(8,128)(2,1)} %param.10) | data formatting | bytes 11811840 | tf_op args[1]
  20.9 16.8 %gather_fusion = bf16[1536,3,769]{2,1,0:T(4,128)(2,1)} fusion(bf16[3,769,1280]{1,0,2:T(4,128)(2,1)} %copy.128, s32[2048]{0:T(1024)S(1)} %pad_clamp_fusion), kind=kCustom, calls=%fused_computation | custom fusion | bytes 14180352 | tf_op jit(solution)/shard_map/jit(_take)/gather | solution.py:165
  37.7 8.5 %copy.129 = bf16[3,769,1536]{1,2,0:T(8,128)(2,1)} copy(bf16[3,769,1536]{1,0,2:T(4,128)(2,1)} %bitcast.161) | data formatting | bytes 14174208 | tf_op jit(solution)/shard_map/jit(_take)/gather | solution.py:165
  46.2 7.5 select_multiply_fusion
  58.5 74.6 %fusion.103 = bf16[1536,2816,1,1]{1,0,3,2:T(8,128)(2,1)S(1)} fusion(s32[1536]{0:T(1024)S(1)} %mul.117, pred[1536]{0:T(1024)(128)(4,1)S(1)} %fusion.74), kind=kLoop, calls=%fused_computation.18.clone.clone.clone.clone.1 | loop fusion | flops 56229888 | bytes 8658432 | tf_op jit(solution)/shard_map/dot_general | solution.py:160
  133.1 10.8 %multiply_convert_fusion.2 = bf16[1536,3,48,8]{0,2,3,1:T(8,128)(2,1)S(1)} fusion(bf16[3,48,8,2816]{3,2,1,0:T(8,128)(2,1)S(1)} %bitcast.166, f32[48]{0:T(128)S(1)} %copy-done.6, bf16[1536,2816,1,1]{1,0,3,2:T(8,128)(2,1)S(1)} %fusion.103), kind=kOutput, calls=%fused_computation.36 | convolution fusion | flops 9969205248 | bytes 18677952 | tf_op jit(solution)/shard_map/dot_general | solution.py:160
  143.9 54.5 %copy.126 = bf16[1536,3,48,8]{3,2,1,0:T(8,128)(2,1)} copy(bf16[1536,3,48,8]{0,2,3,1:T(8,128)(2,1)S(1)} %multiply_convert_fusion.2) | data formatting | bytes 7077888 | tf_op jit(solution)/shard_map/convert_element_type | solution.py:163
  198.3 64.5 %reshape_reshape.10.x = bf16[128,108,128]{2,1,0:T(8,128)(2,1)} reshape(bf16[1536,3,48,8]{3,2,1,0:T(8,128)(2,1)} %copy.126) | data formatting | bytes 7077888 | tf_op jit(solution)/shard_map/reshape;reshape | solution.py:118
  262.9 54.6 %shard_map.91 = bf16[128,108,128]{2,1,0:T(8,128)(2,1)} custom-call(bf16[128,108,128]{2,1,0:T(8,128)(2,1)} %reshape_reshape.10.x), custom_call_target="tpu_custom_call" | custom-call | tf_op jit(solution)/shard_map/pallas_call | solution.py:119
  317.5 70.7 %reshape_reshape.11 = bf16[32,4,3,2,2,3,48,8]{7,6,5,4,3,2,1,0:T(8,128)(2,1)} reshape(bf16[128,108,128]{2,1,0:T(8,128)(2,1)} %shard_map.91) | data formatting | bytes 7077888 | tf_op jit(solution)/shard_map/reshape;reshape | solution.py:177
  388.2 27.8 %fusion.43 = f32[3,4,2,2,3,8,384]{6,5,2,4,3,1,0:T(8,128)S(1)} fusion(bf16[32,4,3,2,2,3,48,8]{7,6,5,4,3,2,1,0:T(8,128)(2,1)} %reshape_reshape.11, bf16[3,769,32,48]{1,3,2,0:T(8,128)(2,1)} %select_multiply_fusion), kind=kOutput, calls=%fused_computation.52 | convolution fusion | flops 1358954496 | bytes 61931520 | tf_op jit(solution)/shard_map/pkgs,glpwcfsd->pwcfldk/dot_general | solution.py:183
  417.2 19.6 %slice.55 = bf16[32,4,3,1,2,3,48,8]{7,6,5,4,3,2,1,0:T(8,128)(2,1)} slice(bf16[32,4,3,2,2,3,48,8]{7,6,5,4,3,2,1,0:T(8,128)(2,1)} %reshape_reshape.11), slice={[0:32], [0:4], [0:3], [0:1], [0:2], [0:3], [0:48], [0:8]} | slice | bytes 3538944 | tf_op jit(solution)/shard_map/slice | solution.py:181
  436.8 21.9 %copy.163 = bf16[32,4,3,1,2,3,48,8]{6,7,0,5,4,1,2,3:T(8,128)(2,1)} copy(bf16[32,4,3,1,2,3,48,8]{7,6,5,4,3,2,1,0:T(8,128)(2,1)} %slice.55) | data formatting | bytes 3538944
  458.7 5.2 fusion.48
  467.2 7.1 convolution_bitcast_fusion
  474.4 9.8 %fusion.31 = bf16[32,4,3,1,2,3,48,8]{6,7,0,1,5,4,3,2:T(8,128)(2,1)} fusion(f32[32,4,3,2,2,3,48,8]{6,7,0,1,5,4,3,2:T(8,128)S(1)} %convolution_bitcast_fusion, bf16[3,769,32,48]{1,3,2,0:T(8,128)(2,1)} %select_multiply_fusion, bf16[3,2,1,4,8,769]{5,4,3,2,1,0:T(8,128)(2,1)S(1)} %fusion.54, bf16[3,2,1,4,8,769]{5,4,3,2,1,0:T(8,128)(2,1)S(1)} %convert_bitcast_fusion, ...), kind=kOutput, calls=%fused_computation.39 | convolution fusion | flops 684346752 | bytes 10912896 | tf_op jit(solution)/shard_map/pkgs,prfldk->glprfsd/dot_general | solution.py:200
  487.2 9.5 %pad_maximum_fusion = bf16[32,4,3,2,2,3,48,8]{6,7,0,1,5,4,3,2:T(8,128)(2,1)} fusion(bf16[32,4,3,1,2,3,48,8]{6,7,0,1,5,4,3,2:T(8,128)(2,1)} %slice.104, bf16[32,4,3,1,2,3,48,8]{6,7,0,1,5,4,3,2:T(8,128)(2,1)} %fusion.31), kind=kLoop, calls=%fused_computation.17 | loop fusion | flops 1769472 | bytes 7077888 | tf_op jit(solution)/shard_map/stack | solution.py:211
  496.7 40.8 %copy.142 = bf16[32,4,3,2,2,3,48,8]{7,6,5,4,3,2,1,0:T(8,128)(2,1)} copy(bf16[32,4,3,2,2,3,48,8]{6,7,0,1,5,4,3,2:T(8,128)(2,1)} %pad_maximum_fusion) | data formatting | bytes 7077888 | tf_op jit(solution)/shard_map/stack | solution.py:211
  537.5 64.5 %convert_element_type.49.x = bf16[128,108,128]{2,1,0:T(8,128)(2,1)} reshape(bf16[32,4,3,2,2,3,48,8]{7,6,5,4,3,2,1,0:T(8,128)(2,1)} %copy.142) | data formatting | bytes 7077888 | tf_op jit(solution)/shard_map/convert_element_type | solution.py:213
  602.1 50.0 %shard_map.92 = bf16[128,108,128]{2,1,0:T(8,128)(2,1)} custom-call(bf16[128,108,128]{2,1,0:T(8,128)(2,1)} %convert_element_type.49.x), custom_call_target="tpu_custom_call" | custom-call | tf_op jit(solution)/shard_map/pallas_call | solution.py:119
  652.1 9.9 %reshape_reshape.12 = bf16[1536,3,384]{2,1,0:T(4,128)(2,1)} reshape(bf16[128,108,128]{2,1,0:T(8,128)(2,1)} %shard_map.92) | data formatting | bytes 7077888 | tf_op jit(solution)/shard_map/reshape;reshape | solution.py:217
  661.9 6.5 copy.143
  669.1 76.5 %fusion.105 = bf16[1536,2816,1,1]{1,0,3,2:T(8,128)(2,1)S(1)} fusion(f32[1536]{0:T(1024)S(1)} %compare_select_fusion.3, s32[1536]{0:T(1024)} %copy-done.1, pred[1536]{0:T(1024)(128)(4,1)} %copy-done.5), kind=kLoop, calls=%fused_computation.19.clone.clone.clone.clone.1 | loop fusion | flops 56229888 | bytes 8664576 | tf_op jit(solution)/shard_map/dot_general | solution.py:218
  745.6 11.9 %fusion.28 = bf16[3,48,8,2816]{3,2,1,0:T(8,128)(2,1)} fusion(bf16[3,384,1536]{2,1,0:T(8,128)(2,1)S(1)} %copy.143, bf16[1536,2816,1,1]{1,0,3,2:T(8,128)(2,1)S(1)} %fusion.105), kind=kOutput, calls=%fused_computation.38 | convolution fusion | flops 9968910336 | bytes 18677760 | tf_op jit(solution)/shard_map/dot_general | solution.py:218
  (63 shorter events, 14.2 us)
Async XLA Ops:
  0.0 464.6 %copy-start = (f32[32,32]{1,0:T(8,128)S(1)}, f32[32,32]{1,0:T(8,128)}, u32[]{:S(2)}) copy-start(f32[32,32]{1,0:T(8,128)} %param.14) | copy-start | bytes 12292
  46.2 9.5 %copy-start.4 = (f32[1280]{0:T(1024)S(1)}, f32[1280]{0:T(1024)}, u32[]{:S(2)}) copy-start(f32[1280]{0:T(1024)} %param.11) | copy-start | bytes 15364
  46.2 10.8 %copy-start.3 = (s32[384]{0:T(512)S(1)}, s32[384]{0:T(512)}, u32[]{:S(2)}) copy-start(s32[384]{0:T(512)} %param.13) | copy-start | bytes 4612
  57.3 0.6 copy-start.1
  57.3 75.8 %copy-start.6 = (f32[48]{0:T(128)S(1)}, f32[48]{0:T(128)}, u32[]{:S(2)}) copy-start(f32[48]{0:T(128)} %compare_select_fusion.4) | copy-start | bytes 580
  57.3 75.8 %slice-start = ((s8[6488064]{0:T(1024)(128)(4,1)}), s8[4194304]{0:T(1024)(128)(4,1)S(1)}, s32[]{:S(2)}) async-start(s8[6488064]{0:T(1024)(128)(4,1)} %bitcast.165), calls=%async_computation | async-start | bytes 8388608
  57.9 0.6 copy-start.5
  58.5 74.6 %slice-start.1 = ((s8[6488064]{0:T(1024)(128)(4,1)}), s8[2293760]{0:T(1024)(128)(4,1)S(1)}, s32[]{:S(2)}) async-start(s8[6488064]{0:T(1024)(128)(4,1)} %bitcast.165), calls=%async_computation.1 | async-start | bytes 4587520
  458.7 5.7 copy-start.7
  458.7 5.7 copy-start.8
  463.9 2.2 copy-start.2

commit v2 on v0

v2 whole, which is shorter than its diff:
```python
import functools
import math

import jax
import jax.numpy as jnp
from jax import lax
from jax.experimental import pallas as pl
from jax.experimental.pallas import tpu as pltpu
from jax.sharding import PartitionSpec as P

WIDTH = 768
NLAT = 1280
POINTS = 2816
ROWS = 784
DEPTH = 896
BANDS = 32
F32, BF16 = jnp.float32, jnp.bfloat16

WINDOWS = ((0, 384), (128, 640), (512, 640), (896, 384))


def swap(a, b, bit, low):
    return (
        jnp.where(low, a, pltpu.roll(b, bit, 1)),
        jnp.where(low, pltpu.roll(a, 128 - bit, 1), b),
    )


def exchange_bits(arrays, base, lane):
    arrays = list(arrays)
    step = 1
    while step < len(arrays):
        bit = base * step
        low = (lane & bit) == 0
        for i in range(len(arrays)):
            if not i & step:
                arrays[i], arrays[i | step] = swap(arrays[i], arrays[i | step], bit, low)
        step *= 2
    return arrays


def lanes_of(rows=16):
    return lax.broadcasted_iota(jnp.int32, (rows, 128), 1)


def cos_sin(value, turn):
    quarter = POINTS // 4
    index = jnp.floor(value * (1.0 / quarter) + 0.5)
    angle = (value - index * quarter) * (2.0 * math.pi / POINTS)
    sq = angle * angle
    c = 1.0 + sq * (-0.5 + sq * (1 / 24 + sq * (-1 / 720 + sq * (1 / 40320))))
    s = angle * (1.0 + sq * (-1 / 6 + sq * (1 / 120 + sq * (-1 / 5040))))
    index = (index.astype(jnp.int32) + turn) & 3
    odd = (index & 1) == 1
    cos = jnp.where(odd, s, c)
    sin = jnp.where(odd, c, s)
    cos = jnp.where((index == 1) | (index == 2), -cos, cos)
    sin = jnp.where(index >= 2, -sin, sin)
    return cos, sin


def make_table(p, wave, part, table, b_cos, b_sin, a_cos, a_sin):
    w = wave[p]
    row = lax.broadcasted_iota(jnp.int32, (128, 512), 0).astype(F32)
    b_cos[...], b_sin[...] = cos_sin(row * w, 0)
    row = lax.broadcasted_iota(jnp.int32, (24, 512), 0).astype(F32)
    a_cos[...], a_sin[...] = cos_sin(row * (128.0 * w), part[p])

    def fill(a, carry):
        values = a_cos[pl.ds(a, 1), :] * b_cos[...] - a_sin[pl.ds(a, 1), :] * b_sin[...]
        table[p, pl.ds(pl.multiple_of(a * 128, 128), 128), :] = values.astype(BF16)
        return carry

    lax.fori_loop(0, POINTS // 128, fill, 0)


def analyse(p, grid, weight, table, y, chunks):
    lane = lanes_of()

    def field(f, carry):
        base = pl.multiple_of(f * 384, 384)
        values = jnp.dot(grid[pl.ds(base, 384), :], table[p], preferred_element_type=F32)
        for tile in range(4):
            y[tile] = values[:, tile * 128 : tile * 128 + 128] * weight[...]

        def chunk(n, carry):
            third, tile = n // 4, lax.rem(n, 4)
            levels = [y[tile, pl.ds(third * 128 + l, 16, stride=8), :] for l in range(8)]
            for e, out in enumerate(exchange_bits(levels, 1, lane)):
                chunks[9 * p + 3 * f + third, tile * 8 + e] = out.astype(BF16)
            return carry

        return lax.fori_loop(0, 12, chunk, carry)

    lax.fori_loop(0, 3, field, 0)


def pack_chunks(t, chunks, send):
    lane = lanes_of()

    def group(i, carry):
        parts = [chunks[4 * t + g, i].astype(F32) for g in range(4)]
        for x, out in enumerate(exchange_bits(parts, 32, lane)):
            send[4 * i + x, t] = out.astype(BF16)
        return carry

    lax.fori_loop(0, BANDS, group, 0)


def forward_kernel(grid, wave, part, weight, send, table, b_cos, b_sin, a_cos, a_sin, y, chunks):
    chunks[27] = jnp.zeros(chunks.shape[1:], BF16)
    for p in range(3):
        make_table(p, wave, part, table, b_cos, b_sin, a_cos, a_sin)
        analyse(p, grid, weight, table, y, chunks)
        for t in range(2 * p, 2 * p + (3 if p == 2 else 2)):
            pack_chunks(t, chunks, send)


def spread_legendre(p, legendre, slot_row, slot_column, wide, tall):
    wide[p, 768:ROWS, :] = jnp.zeros((16, 1536), BF16)
    tall[p, :, 768:DEPTH] = jnp.zeros((1536, 128), BF16)
    for tile, (low, size) in enumerate(WINDOWS):
        at = tile * 384
        part = legendre[p, :, low : low + size]
        row = lax.broadcasted_iota(jnp.int32, (size, 384), 0) + low
        pick = jnp.where(row == slot_row[:, at : at + 384], 1.0, 0.0).astype(BF16)
        wide[p, 0 : WIDTH + 1, at : at + 384] = jnp.dot(
            part, pick, preferred_element_type=F32
        ).astype(BF16)
        row = lax.broadcasted_iota(jnp.int32, (384, size), 1) + low
        pick = jnp.where(row == slot_column[at : at + 384, :], 1.0, 0.0).astype(BF16)
        tall[p, at : at + 384, 0 : WIDTH + 1] = lax.dot_general(
            pick, part, (((1,), (1,)), ((), ())), preferred_element_type=F32
        ).astype(BF16)


def gather_tiles(t, received, fourier):
    lane = lanes_of()

    def band(b, carry):
        parts = [received[4 * b + v, t].astype(F32) for v in range(4)]
        for g, out in enumerate(exchange_bits(parts, 32, lane)):
            q = 4 * t + g
            if q < 27:
                f, third = q % 9 // 3, q % 3
                row = pl.multiple_of(b * 48 + third * 16, 16)
                fourier[q // 9, pl.ds(row, 16), f * 128 : f * 128 + 128] = out.astype(BF16)
        return carry

    lax.fori_loop(0, BANDS, band, 0)


def spectral_step(p, own_wave, lane_scales, mixes, wide, tall, fourier, spectral, updated, synthesis):
    wave = own_wave[p]
    spectral[...] = jnp.dot(wide[p], fourier[p], preferred_element_type=F32)
    exact = functools.partial(
        jnp.dot, precision=lax.Precision.HIGHEST, preferred_element_type=F32
    )
    upper = (lanes_of(112) & 16) != 0
    updated[ROWS:DEPTH, :] = jnp.zeros((DEPTH - ROWS, 384), BF16)

    def block(i, carry):
        at = pl.multiple_of(i * 112, 112)
        k = lax.broadcasted_iota(jnp.int32, (112, 128), 0) + at
        own = k < WIDTH - wave
        degree = jnp.where(own, wave + k, k - 1)
        ratio = (degree * (degree + 1)).astype(F32) / float(WIDTH * (WIDTH - 1))
        keep = (own != upper) & (k <= WIDTH)
        rows = pl.ds(at, 112)
        first = spectral[rows, 0:128] / (1.0 + lane_scales[0:1, :] * ratio * ratio)
        modes = exact(spectral[rows, 128:256], mixes[0])
        modes = modes / (1.0 + lane_scales[1:2, :] * ratio)
        second = exact(modes, mixes[1])
        third = spectral[rows, 256:384] - exact(second, mixes[2])
        for f, values in enumerate((first, second, third)):
            updated[rows, f * 128 : f * 128 + 128] = jnp.where(keep, values, 0.0).astype(BF16)
        return carry

    lax.fori_loop(0, ROWS // 112, block, 0)
    double = (lax.broadcasted_iota(jnp.int32, (1, 384), 1) & 16 != 0) | (wave > 0)
    factor = jnp.where(double, 2.0, 1.0)

    def rows_of(i, carry):
        at = pl.multiple_of(i * 384, 384)
        values = jnp.dot(tall[p, pl.ds(at, 384), :], updated[...], preferred_element_type=F32)
        synthesis[p, pl.ds(at, 384), :] = (values * factor).astype(BF16)
        return carry

    lax.fori_loop(0, 4, rows_of, 0)


def scatter_tiles(t, synthesis, send):
    lane = lanes_of()

    def band(b, carry):
        parts = []
        for g in range(4):
            q = min(4 * t + g, 26)
            f, third = q % 9 // 3, q % 3
            row = pl.multiple_of(b * 48 + third * 16, 16)
            parts.append(
                synthesis[q // 9, pl.ds(row, 16), f * 128 : f * 128 + 128].astype(F32)
            )
        for v, out in enumerate(exchange_bits(parts, 32, lane)):
            send[4 * b + v, t] = out.astype(BF16)
        return carry

    lax.fori_loop(0, BANDS, band, 0)


def middle_kernel(
    received, legendre, slot_row, slot_column, own_wave, lane_scales, mixes,
    send, wide, tall, fourier, spectral, updated, synthesis,
):
    for p in range(3):
        spread_legendre(p, legendre, slot_row, slot_column, wide, tall)
    for t in range(7):
        gather_tiles(t, received, fourier)
    for p in range(3):
        spectral_step(
            p, own_wave, lane_scales, mixes, wide, tall, fourier, spectral, updated, synthesis
        )
    for t in range(7):
        scatter_tiles(t, synthesis, send)


def open_tiles(t, received, chunks):
    lane = lanes_of()

    def group(i, carry):
        parts = [received[4 * i + x, t].astype(F32) for x in range(4)]
        for g, out in enumerate(exchange_bits(parts, 32, lane)):
            if 4 * t + g < 27:
                chunks[4 * t + g, i] = out.astype(BF16)
        return carry

    lax.fori_loop(0, BANDS, group, 0)


def synthesise(f, chunks, table, y, columns, out):
    lane = lanes_of()

    def chunk(n, carry):
        tile, third = n // 3, lax.rem(n, 3)
        p, eighth = tile // 4, lax.rem(tile, 4)
        parts = [chunks[9 * p + 3 * f + third, eighth * 8 + e].astype(F32) for e in range(8)]
        for l, values in enumerate(exchange_bits(parts, 1, lane)):
            y[tile, pl.ds(third * 128 + l, 16, stride=8), :] = values
        return carry

    lax.fori_loop(0, 36, chunk, 0)
    for tile in range(12):
        columns[:, tile * 128 : tile * 128 + 128] = y[tile].astype(BF16)
    base = pl.multiple_of(f * 384, 384)

    def points(i, carry):
        at = pl.multiple_of(i * 256, 256)
        total = jnp.zeros((384, 256), F32)
        for p in range(3):
            total = total + lax.dot_general(
                columns[:, p * 512 : p * 512 + 512],
                table[p, pl.ds(at, 256), :],
                (((1,), (1,)), ((), ())),
                preferred_element_type=F32,
            )
        out[pl.ds(base, 384), pl.ds(at, 256)] = total.astype(BF16)
        return carry

    lax.fori_loop(0, POINTS // 256, points, 0)


def inverse_kernel(received, table, out, y, columns, chunks):
    for t in range(7):
        open_tiles(t, received, chunks)

    def field(f, carry):
        synthesise(f, chunks, table, y, columns, out)
        return carry

    lax.fori_loop(0, 3, field, 0)


def call(kernel, inputs, spaces, outs, scratch, **params):
    vmem = pl.BlockSpec(memory_space=pltpu.VMEM)
    smem = pl.BlockSpec(memory_space=pltpu.SMEM)
    return pl.pallas_call(
        kernel,
        out_shape=[jax.ShapeDtypeStruct(s, d) for s, d in outs],
        in_specs=[smem if s == "s" else vmem for s in spaces],
        out_specs=[vmem] * len(outs),
        scratch_shapes=[pltpu.VMEM(s, d) for s, d in scratch],
        compiler_params=pltpu.CompilerParams(vmem_limit_bytes=62 * 2**20, **params),
    )(*inputs)


def shards(
    grid,
    legendre,
    gauss_weights,
    band_counts,
    pair_m,
    vert_modes,
    mode_depth,
    diffusion,
    pressure_balance_matrix,
):
    lev_groups = 4
    fields, lat_cap, lev_dev, points = grid.shape
    my_band = lax.axis_index("lat")
    owner = my_band * lev_groups + lax.axis_index("lev")
    band_starts = jnp.cumsum(band_counts) - band_counts
    offsets = jnp.arange(lat_cap, dtype=jnp.int32)
    slot = jnp.where(
        offsets[None, :] < band_counts[:, None], band_starts[:, None] + offsets[None, :], -1
    ).astype(jnp.int32)
    my_start = lax.dynamic_slice(band_starts, (my_band,), (1,))[0]
    my_count = lax.dynamic_slice(band_counts, (my_band,), (1,))[0]
    padded = jnp.concatenate([gauss_weights, jnp.zeros((lat_cap,), F32)])
    weight = lax.dynamic_slice(padded, (my_start,), (lat_cap,)) * (1.0 / POINTS)
    weight = jnp.where(offsets < my_count, weight, 0.0)
    weight = jnp.broadcast_to(weight[:, None, None], (lat_cap, lev_dev, 128)).reshape(384, 128)

    lower = pair_m.reshape(4, 8, 4, 3).transpose(3, 0, 2, 1)
    waves = jnp.stack([lower, WIDTH - 1 - lower], axis=3)
    waves = jnp.broadcast_to(waves[:, :, :, :, None, :], (3, 4, 4, 2, 2, 8))
    part = jnp.broadcast_to(
        jnp.arange(2, dtype=jnp.int32)[None, None, None, None, :, None], waves.shape
    ).reshape(3, 1, 512)
    waves = waves.reshape(3, 1, 512).astype(F32)
    own_wave = lax.dynamic_slice(pair_m, (owner * 3,), (3,))

    def over_lanes(v):
        v = v.reshape(4, 1, 8)
        return jnp.broadcast_to(v, (4, 4, 8)).reshape(128)

    def mix(m):
        m = m.reshape(4, 1, 8, 4, 1, 8) * jnp.eye(4, dtype=F32).reshape(1, 4, 1, 1, 4, 1)
        return m.reshape(128, 128)

    lane_scales = jnp.stack([over_lanes(diffusion), over_lanes(mode_depth)])
    mixes = jnp.stack([mix(vert_modes.T), mix(vert_modes), mix(pressure_balance_matrix.T)])

    block = (128, 7, 16, 128)
    small = [((128, 512), F32)] * 2 + [((24, 512), F32)] * 2
    send, table = call(
        forward_kernel,
        (grid.reshape(1152, points), waves, part, weight),
        "vvvv",
        [(block, BF16), ((3, points, 512), BF16)],
        small + [((4, 384, 128), F32), ((28, 32, 16, 128), BF16)],
    )
    received = lax.all_to_all(send, ("lat", "lev"), 0, 0, tiled=True)
    (send,) = call(
        middle_kernel,
        (received, legendre, slot.reshape(1, 1536), slot.reshape(1536, 1), own_wave, lane_scales, mixes),
        "vvvvsvv",
        [(block, BF16)],
        [
            ((3, ROWS, 1536), BF16),
            ((3, 1536, DEPTH), BF16),
            ((3, 1536, 384), BF16),
            ((ROWS, 384), F32),
            ((DEPTH, 384), BF16),
            ((3, 1536, 384), BF16),
        ],
    )
    received = lax.all_to_all(send, ("lat", "lev"), 0, 0, tiled=True)
    (out,) = call(
        inverse_kernel,
        (received, table),
        "vv",
        [((1152, points), BF16)],
        [((12, 384, 128), F32), ((384, 1536), BF16), ((28, 32, 16, 128), BF16)],
    )
    return out.reshape(fields, lat_cap, lev_dev, points)


def solution(mesh):
    placed = (
        P(None, "lat", "lev", None),
        P(("lat", "lev"), None, None),
        P(),
        P(),
        P(),
        P(),
        P(),
        P(),
        P(),
    )
    return jax.shard_map(
        shards, mesh=mesh, in_specs=placed, out_specs=P(None, "lat", "lev", None), check_vma=False
    )
```

time: 709 us -> 394 us (0.56); the launches traced: 695 us -> 394 us
  local copies, waits for them, and re-layouts: 415 us -> 13.7 us
  Pallas kernels: 0 us -> 271 us
  other arithmetic: 176 us -> 4.44 us
  matrix products: 79.1 us -> 0 us
  blocking collectives: 0 us -> 52.5 us
  waiting for transfers between devices: 4.64 us -> 37.6 us
    pallas_call x0 -> x3, Pallas kernels: none -> 271 us  [call(): pl.pallas_call(kernel, out_shape=[jax.ShapeDtypeStruct(s, d) for s, d in...]
    reshape x3 -> x1, local copies, waits for them, and re-layouts: 201 us -> 0.93 us  [shards(): lower = pair_m.reshape(4, 8, 4, 3).transpose(3, 0, 2, 1)]
    dot_general x2 -> x0, other arithmetic: 151 us -> none  [the longest x1 76.2 us: shards(): lax.dot_general(columns, inverse_table, (((0,), (0,)), ((), ())), preferr...]
    convert_element_type x3 -> x2, local copies, waits for them, and re-layouts: 115 us -> 0.8 us  [shards(): waves = waves.reshape(3, 1, 512).astype(F32)]
    dot_general x9 -> x0, matrix products: 79.1 us -> none  [the longest x1 27.1 us: shards(): jnp.einsum('pkgs,glpwcfsd->pwcfldk', table_tail, arranged, preferred_elem...]
    all_to_all x0 -> x1, blocking collectives: none -> 52.5 us  [shards(): received = lax.all_to_all(send, ('lat', 'lev'), 0, 0, tiled=True)]
    unnamed x32 -> x10, local copies, waits for them, and re-layouts: 39.7 us -> 0.02 us
    all_to_all x2 -> x1, waiting for transfers between devices: 4.64 us -> 37.6 us  [shards(): received = lax.all_to_all(send, ('lat', 'lev'), 0, 0, tiled=True)]
  transfers between devices with their start and end apart: 2 -> 1, of which waited for: 1 -> 1; matrix products, arithmetic and copies ran while one was open for 19% -> 2% of each run, Pallas kernels for 0% -> 0%
where the time goes in v2:
time: 394 us
  Pallas kernels  271 us (69%)
  blocking collectives  52.5 us (13%)
  waiting for transfers between devices  37.6 us (10%)
  local copies, waits for them, and re-layouts  13.7 us (3%)
  starting transfers between devices  12.1 us (3%)
  other arithmetic  4.44 us (1%)
    pallas_call x3, Pallas kernels, call(): pl.pallas_call(kernel, out_shape=[jax.ShapeDtypeStruct(s, d) for s, d in...  271 us
    all_to_all x1, blocking collectives, shards(): received = lax.all_to_all(send, ('lat', 'lev'), 0, 0, tiled=True)  52.5 us
    all_to_all x1, waiting for transfers between devices, shards(): received = lax.all_to_all(send, ('lat', 'lev'), 0, 0, tiled=True)  37.6 us
    all_to_all x1, starting transfers between devices, shards(): received = lax.all_to_all(send, ('lat', 'lev'), 0, 0, tiled=True)  12.1 us
  transfers between devices with their start and end apart: 1, of which 1 were waited for; matrix products, arithmetic and copies ran while one was open for 2% of the time, Pallas kernels for 0%

profile of v2, /device:TPU:1, one launch (start us, length us, event | category | flops | bytes accessed | tf_op | source)
XLA Modules:
  0.0 393.8 jit_solution(2558116661482604105)
XLA Ops:
  0.0 1.3 dynamic_slice.12
  1.3 0.7 copy.22
  2.2 0.7 sub.11
  2.8 0.6 dynamic_slice.13
  5.4 1.4 compare_select_fusion
  7.0 0.9 reshape.245
  8.5 0.8 convert_element_type.19.wave
  9.2 0.6 broadcast_in_dim.56.part
  9.8 0.8 broadcast_in_dim.60.weight
  10.6 80.4 %shard_map.91 = (bf16[128,7,16,128]{3,2,1,0:T(8,128)(2,1)}, bf16[3,2816,512]{2,1,0:T(8,128)(2,1)}) custom-call(bf16[1152,2816]{1,0:T(8,128)(2,1)} %bitcast.19, f32[3,1,512]{2,1,0:T(1,128)} %convert_element_type.19.wave, s32[3,1,512]{2,1,0:T(1,128)} %broadcast_in_dim.56.part, f32[384,128]{1,0:T(8,128)} %broadcast_in_dim.60.weight), custom_call_target="tpu_custom_call" | custom-call | tf_op jit(solution)/shard_map/pallas_call | solution.py:286
  91.1 12.1 %all-to-all-start = ((bf16[128,7,16,128]{3,2,1,0:T(8,128)(2,1)}), bf16[128,7,16,128]{3,2,1,0:T(8,128)(2,1)}, u32[]{:S(2)}, u32[]{:S(2)}) async-start(bf16[128,7,16,128]{3,2,1,0:T(8,128)(2,1)} %get-tuple-element.7), calls=%async_computation | async-start | bytes 7340032 | tf_op jit(solution)/shard_map/all_to_all | solution.py:352
  103.2 0.7 select_n.42.slot_row
  103.9 1.3 select_n.45.slot_column
  105.2 1.3 dynamic_slice.15.own_wave
  107.4 0.8 broadcast_multiply_fusion.2
  108.2 1.0 mul.95
  109.3 1.0 mul.99
  110.3 1.0 mul.103
  111.4 0.6 pad_maximum_fusion.1.lane_scales
  112.0 0.7 pad_maximum_fusion.mixes
  112.7 37.6 %all-to-all-done.received = bf16[128,7,16,128]{3,2,1,0:T(8,128)(2,1)} async-done(((bf16[128,7,16,128]{3,2,1,0:T(8,128)(2,1)}), bf16[128,7,16,128]{3,2,1,0:T(8,128)(2,1)}, u32[]{:S(2)}, u32[]{:S(2)}) %all-to-all-start) | async-done | bytes 3670048 | tf_op jit(solution)/shard_map/all_to_all | solution.py:352
  150.3 108.0 %shard_map.92 = bf16[128,7,16,128]{3,2,1,0:T(8,128)(2,1)} custom-call(bf16[128,7,16,128]{3,2,1,0:T(8,128)(2,1)} %all-to-all-done.received, bf16[3,769,1280]{2,1,0:T(8,128)(2,1)} %legendre.1, s32[1,1536]{1,0:T(1,128)} %select_n.42.slot_row, s32[1536,1]{1,0:T(8,128)} %select_n.45.slot_column, s32[3]{0:T(128)} %dynamic_slice.15.own_wave, ...), custom_call_target="tpu_custom_call" | custom-call | tf_op jit(solution)/shard_map/pallas_call | solution.py:286
  258.2 52.5 %all_to_all.10.received = bf16[128,7,16,128]{3,2,1,0:T(8,128)(2,1)} all-to-all(bf16[128,7,16,128]{3,2,1,0:T(8,128)(2,1)} %shard_map.92), channel_id=1, replica_groups=mesh['lat'=32,'lev'=4] {'lat','lev'}, dimensions={0} | all-to-all | bytes 7340032 | tf_op jit(solution)/shard_map/all_to_all | solution.py:367
  310.8 83.1 %shard_map.93 = bf16[1152,2816]{1,0:T(8,128)(2,1)} custom-call(bf16[128,7,16,128]{3,2,1,0:T(8,128)(2,1)} %all_to_all.10.received, bf16[3,2816,512]{2,1,0:T(8,128)(2,1)} %get-tuple-element.8.table), custom_call_target="tpu_custom_call" | custom-call | tf_op jit(solution)/shard_map/pallas_call | solution.py:286
  (35 shorter events, 1.8 us)
Async XLA Ops:
  10.6 92.5 %copy-start.2 = (s32[32]{0:T(128)S(1)}, s32[32]{0:T(128)}, u32[]{:S(2)}) copy-start(s32[32]{0:T(128)} %param.12) | copy-start | bytes 388
  10.6 95.9 %copy-start.3 = (f32[32]{0:T(128)S(1)}, f32[32]{0:T(128)}, u32[]{:S(2)}) copy-start(f32[32]{0:T(128)} %param.15) | copy-start | bytes 388
  10.6 96.0 %copy-start.4 = (f32[32]{0:T(128)S(1)}, f32[32]{0:T(128)}, u32[]{:S(2)}) copy-start(f32[32]{0:T(128)} %param.16) | copy-start | bytes 388
  10.6 96.3 %copy-start.1 = (f32[32,32]{1,0:T(8,128)S(1)}, f32[32,32]{1,0:T(8,128)}, u32[]{:S(2)}) copy-start(f32[32,32]{1,0:T(8,128)} %param.17) | copy-start | bytes 12292
  10.6 96.5 %copy-start = (f32[32,32]{1,0:T(8,128)S(1)}, f32[32,32]{1,0:T(8,128)}, u32[]{:S(2)}) copy-start(f32[32,32]{1,0:T(8,128)} %param.14) | copy-start | bytes 12292
  91.1 59.2 %all-to-all-start = ((bf16[128,7,16,128]{3,2,1,0:T(8,128)(2,1)}), bf16[128,7,16,128]{3,2,1,0:T(8,128)(2,1)}, u32[]{:S(2)}, u32[]{:S(2)}) async-start(bf16[128,7,16,128]{3,2,1,0:T(8,128)(2,1)} %get-tuple-element.7), calls=%async_computation | async-start | bytes 7340032 | tf_op jit(solution)/shard_map/all_to_all | solution.py:352

commit v3 on v2

v3 whole, which is shorter than its diff:
```python
import math

import jax
import jax.numpy as jnp
from jax import lax
from jax.experimental import pallas as pl
from jax.experimental.pallas import tpu as pltpu
from jax.sharding import PartitionSpec as P

WIDTH = 768
NLAT = 1280
POINTS = 2816
ROWS = 784
DEPTH = 896
BANDS = 32
F32, BF16 = jnp.float32, jnp.bfloat16

WINDOWS = ((0, 384), (128, 640), (512, 640), (896, 384))


def swap(a, b, bit, low):
    return (
        jnp.where(low, a, pltpu.roll(b, bit, 1)),
        jnp.where(low, pltpu.roll(a, 128 - bit, 1), b),
    )


def exchange_bits(arrays, base, lane):
    arrays = list(arrays)
    step = 1
    while step < len(arrays):
        bit = base * step
        low = (lane & bit) == 0
        for i in range(len(arrays)):
            if not i & step:
                arrays[i], arrays[i | step] = swap(arrays[i], arrays[i | step], bit, low)
        step *= 2
    return arrays


def each(total, together, load, base, store):
    lane = lanes_of()

    def body(i, carry):
        groups = [load(i * together + u) for u in range(together)]
        groups = [exchange_bits(parts, base, lane) for parts in groups]
        for u, parts in enumerate(groups):
            store(i * together + u, parts)
        return carry

    lax.fori_loop(0, total // together, body, 0)


def lanes_of(rows=16):
    return lax.broadcasted_iota(jnp.int32, (rows, 128), 1)


def cos_sin(value, turn):
    quarter = POINTS // 4
    index = jnp.floor(value * (1.0 / quarter) + 0.5)
    angle = (value - index * quarter) * (2.0 * math.pi / POINTS)
    sq = angle * angle
    c = 1.0 + sq * (-0.5 + sq * (1 / 24 + sq * (-1 / 720 + sq * (1 / 40320))))
    s = angle * (1.0 + sq * (-1 / 6 + sq * (1 / 120 + sq * (-1 / 5040))))
    index = (index.astype(jnp.int32) + turn) & 3
    odd = (index & 1) == 1
    cos = jnp.where(odd, s, c)
    sin = jnp.where(odd, c, s)
    cos = jnp.where((index == 1) | (index == 2), -cos, cos)
    sin = jnp.where(index >= 2, -sin, sin)
    return cos, sin


def make_table(p, wave, part, table, b_cos, b_sin, a_cos, a_sin):
    w = wave[p]
    row = lax.broadcasted_iota(jnp.int32, (128, 512), 0).astype(F32)
    b_cos[...], b_sin[...] = cos_sin(row * w, 0)
    row = lax.broadcasted_iota(jnp.int32, (24, 512), 0).astype(F32)
    a_cos[...], a_sin[...] = cos_sin(row * (128.0 * w), part[p])

    def fill(a, carry):
        values = a_cos[pl.ds(a, 1), :] * b_cos[...] - a_sin[pl.ds(a, 1), :] * b_sin[...]
        table[p, pl.ds(pl.multiple_of(a * 128, 128), 128), :] = values.astype(BF16)
        return carry

    lax.fori_loop(0, POINTS // 128, fill, 0)


def analyse(p, grid, weight, table, y, chunks):
    def field(f, carry):
        base = pl.multiple_of(f * 384, 384)
        values = jnp.dot(grid[pl.ds(base, 384), :], table[p], preferred_element_type=F32)
        for tile in range(4):
            y[tile] = values[:, tile * 128 : tile * 128 + 128] * weight[...]

        def load(n):
            third, tile = n // 4, lax.rem(n, 4)
            return [
                y[tile, pl.ds(third * 128 + l, 16, stride=8), :].astype(BF16) for l in range(8)
            ]

        def store(n, parts):
            third, tile = n // 4, lax.rem(n, 4)
            for e, out in enumerate(parts):
                chunks[9 * p + 3 * f + third, tile * 8 + e] = out

        each(12, 4, load, 1, store)
        return carry

    lax.fori_loop(0, 3, field, 0)


def pack_chunks(t, chunks, send):
    def load(i):
        return [chunks[4 * t + g, i] for g in range(4)]

    def store(i, parts):
        for x, out in enumerate(parts):
            send[4 * i + x, t] = out

    each(BANDS, 8, load, 32, store)


def spread_legendre(p, legendre, slot_row, slot_column, wide, tall):
    wide[p, 768:ROWS, :] = jnp.zeros((16, 1536), BF16)
    tall[p, :, 768:DEPTH] = jnp.zeros((1536, 128), BF16)
    for tile, (low, size) in enumerate(WINDOWS):
        at = tile * 384
        part = legendre[p, :, low : low + size]
        row = lax.broadcasted_iota(jnp.int32, (size, 384), 0) + low
        pick = jnp.where(row == slot_row[:, at : at + 384], 1.0, 0.0).astype(BF16)
        wide[p, 0 : WIDTH + 1, at : at + 384] = jnp.dot(
            part, pick, preferred_element_type=F32
        ).astype(BF16)
        row = lax.broadcasted_iota(jnp.int32, (384, size), 1) + low
        pick = jnp.where(row == slot_column[at : at + 384, :], 1.0, 0.0).astype(BF16)
        tall[p, at : at + 384, 0 : WIDTH + 1] = lax.dot_general(
            pick, part, (((1,), (1,)), ((), ())), preferred_element_type=F32
        ).astype(BF16)


def gather_tiles(t, received, fourier):
    def load(b):
        return [received[4 * b + v, t] for v in range(4)]

    def store(b, parts):
        for g, out in enumerate(parts):
            q = 4 * t + g
            if q < 27:
                f, third = q % 9 // 3, q % 3
                row = pl.multiple_of(b * 48 + third * 16, 16)
                fourier[q // 9, pl.ds(row, 16), f * 128 : f * 128 + 128] = out

    each(BANDS, 8, load, 32, store)


def split_mix(i, mixes, mixers):
    mix = mixes[i]
    high = mix.astype(BF16)
    mixers[i, 0:128, 0:128] = high
    mixers[i, 128:256, 0:128] = high
    mixers[i, 0:128, 128:256] = (mix - high.astype(F32)).astype(BF16)
    mixers[i, 128:256, 128:256] = jnp.zeros((128, 128), BF16)


def mixed(values, mixer):
    high = values.astype(BF16)
    low = (values - high.astype(F32)).astype(BF16)
    out = jnp.dot(
        jnp.concatenate([high, low], axis=1), mixer, preferred_element_type=F32
    )
    return out[:, 0:128] + out[:, 128:256]


def spectral_step(p, own_wave, lane_scales, mixers, wide, tall, fourier, spectral, updated):
    wave = own_wave[p]
    spectral[...] = jnp.dot(wide[p], fourier[p], preferred_element_type=F32)
    upper = (lanes_of(112) & 16) != 0
    updated[ROWS:DEPTH, :] = jnp.zeros((DEPTH - ROWS, 384), BF16)

    def block(i, carry):
        at = pl.multiple_of(i * 112, 112)
        k = lax.broadcasted_iota(jnp.int32, (112, 128), 0) + at
        own = k < WIDTH - wave
        degree = jnp.where(own, wave + k, k - 1)
        ratio = (degree * (degree + 1)).astype(F32) / float(WIDTH * (WIDTH - 1))
        keep = (own != upper) & (k <= WIDTH)
        rows = pl.ds(at, 112)
        first = spectral[rows, 0:128] / (1.0 + lane_scales[0:1, :] * ratio * ratio)
        modes = mixed(spectral[rows, 128:256], mixers[0])
        modes = modes / (1.0 + lane_scales[1:2, :] * ratio)
        second = mixed(modes, mixers[1])
        third = spectral[rows, 256:384] - mixed(second, mixers[2])
        for f, values in enumerate((first, second, third)):
            updated[rows, f * 128 : f * 128 + 128] = jnp.where(keep, values, 0.0).astype(BF16)
        return carry

    lax.fori_loop(0, ROWS // 112, block, 0)
    double = (lax.broadcasted_iota(jnp.int32, (1, 384), 1) & 16 != 0) | (wave > 0)
    factor = jnp.where(double, 2.0, 1.0)

    def rows_of(i, carry):
        at = pl.multiple_of(i * 384, 384)
        values = jnp.dot(tall[p, pl.ds(at, 384), :], updated[...], preferred_element_type=F32)
        fourier[p, pl.ds(at, 384), :] = (values * factor).astype(BF16)
        return carry

    lax.fori_loop(0, 4, rows_of, 0)


def scatter_tiles(t, synthesis, send):
    def load(b):
        parts = []
        for g in range(4):
            q = min(4 * t + g, 26)
            f, third = q % 9 // 3, q % 3
            row = pl.multiple_of(b * 48 + third * 16, 16)
            parts.append(synthesis[q // 9, pl.ds(row, 16), f * 128 : f * 128 + 128])
        return parts

    def store(b, parts):
        for v, out in enumerate(parts):
            send[4 * b + v, t] = out

    each(BANDS, 8, load, 32, store)


def open_tiles(t, received, chunks):
    def load(i):
        return [received[4 * i + x, t] for x in range(4)]

    def store(i, parts):
        for g, out in enumerate(parts):
            if 4 * t + g < 27:
                chunks[4 * t + g, i] = out

    each(BANDS, 8, load, 32, store)


def synthesise(f, chunks, table, y, columns, out):
    def load(n):
        tile, third = n // 3, lax.rem(n, 3)
        p, eighth = tile // 4, lax.rem(tile, 4)
        return [chunks[9 * p + 3 * f + third, eighth * 8 + e] for e in range(8)]

    def store(n, parts):
        tile, third = n // 3, lax.rem(n, 3)
        for l, values in enumerate(parts):
            y[tile, pl.ds(third * 128 + l, 16, stride=8), :] = values.astype(F32)

    each(36, 4, load, 1, store)
    for tile in range(12):
        columns[:, tile * 128 : tile * 128 + 128] = y[tile].astype(BF16)
    base = pl.multiple_of(f * 384, 384)

    def points(i, carry):
        at = pl.multiple_of(i * 256, 256)
        total = jnp.zeros((384, 256), F32)
        for p in range(3):
            total = total + lax.dot_general(
                columns[:, p * 512 : p * 512 + 512],
                table[p, pl.ds(at, 256), :],
                (((1,), (1,)), ((), ())),
                preferred_element_type=F32,
            )
        out[pl.ds(base, 384), pl.ds(at, 256)] = total.astype(BF16)
        return carry

    lax.fori_loop(0, POINTS // 256, points, 0)


PHASES = ((0, 2), (2, 2), (4, 3))


def place():
    lat, lev = lax.axis_index("lat"), lax.axis_index("lev")
    return lat, lev, lat * 4 + lev


def partner(k, lat, lev):
    step = lax.rem(k * 37, 128)
    z = lax.rem(lat // 8 + step // 32, 4)
    y = lax.rem(lat // 2 + step // 8, 4)
    core = lax.rem(lat + step, 2)
    return (z * 4 + y) * 2 + core, lax.rem(lev + step // 2, 4)


def greet_all():
    lat, lev, _ = place()
    barrier = pltpu.get_barrier_semaphore()

    def greet(k, carry):
        pl.semaphore_signal(
            barrier,
            inc=1,
            device_id=partner(k, lat, lev),
            device_id_type=pl.DeviceIdType.MESH,
        )
        return carry

    lax.fori_loop(1, 128, greet, 0)


def launch(phase, send, received, send_sem, recv_sem, own_sem):
    lat, lev, me = place()
    first, count = PHASES[phase]
    tiles = pl.ds(first, count)
    pltpu.make_async_copy(send.at[me, tiles], received.at[me, tiles], own_sem).start()

    def one(k, carry):
        to = partner(k, lat, lev)
        pltpu.make_async_remote_copy(
            src_ref=send.at[to[0] * 4 + to[1], tiles],
            dst_ref=received.at[me, tiles],
            send_sem=send_sem,
            recv_sem=recv_sem,
            device_id=to,
            device_id_type=pl.DeviceIdType.MESH,
        ).start()
        return carry

    lax.fori_loop(1, 128, one, 0)


def rest(phase, send, received, send_sem, recv_sem):
    lat, lev, _ = place()
    first, count = PHASES[phase]
    others = pl.ds(0, 127), pl.ds(first, count)
    return pltpu.make_async_remote_copy(
        src_ref=send.at[others],
        dst_ref=received.at[others],
        send_sem=send_sem,
        recv_sem=recv_sem,
        device_id=(lat, lev),
        device_id_type=pl.DeviceIdType.MESH,
    )


def arrive(phase, send, received, send_sem, recv_sem, own_sem):
    _, _, me = place()
    first, count = PHASES[phase]
    tiles = pl.ds(first, count)
    pltpu.make_async_copy(send.at[me, tiles], received.at[me, tiles], own_sem).wait()
    rest(phase, send, received, send_sem, recv_sem).wait_recv()


def step_kernel(
    grid_hbm, legendre_hbm, wave, part, weight, slot_row, slot_column, own_wave, lane_scales, mixes,
    out_hbm,
    grid, legendre, table, b_cos, b_sin, a_cos, a_sin, y, columns, chunks, send, received, returned,
    wide, tall, fourier, spectral, updated, mixers,
    grid_sem, legendre_sem, out_sem, send_sem, recv_sem, own_sem,
):
    def field_of(ref, f):
        return ref.at[pl.ds(f * 384, 384)]

    for f in range(3):
        pltpu.make_async_copy(field_of(grid_hbm, f), field_of(grid, f), grid_sem.at[f]).start()
    pltpu.make_async_copy(legendre_hbm, legendre, legendre_sem).start()
    greet_all()
    chunks[27] = jnp.zeros(chunks.shape[1:], BF16)
    there = [
        (send, received, send_sem.at[i], recv_sem.at[i], own_sem.at[i]) for i in range(3)
    ]
    back = [
        (send, returned, send_sem.at[3 + i], recv_sem.at[3 + i], own_sem.at[3 + i])
        for i in range(3)
    ]
    for p in range(3):
        make_table(p, wave, part, table, b_cos, b_sin, a_cos, a_sin)
        if p == 0:
            for f in range(3):
                pltpu.make_async_copy(
                    field_of(grid_hbm, f), field_of(grid, f), grid_sem.at[f]
                ).wait()
        analyse(p, grid, weight, table, y, chunks)
        first, count = PHASES[p]
        for t in range(first, first + count):
            pack_chunks(t, chunks, send)
        if p == 0:
            pl.semaphore_wait(pltpu.get_barrier_semaphore(), 127)
        launch(p, *there[p])
    pltpu.make_async_copy(legendre_hbm, legendre, legendre_sem).wait()
    for i in range(3):
        split_mix(i, mixes, mixers)
    for p in range(3):
        spread_legendre(p, legendre, slot_row, slot_column, wide, tall)
    for p in range(3):
        for phase in ((0, 1), (2,), ())[p]:
            arrive(phase, *there[phase])
            first, count = PHASES[phase]
            for t in range(first, first + count):
                gather_tiles(t, received, fourier)
        spectral_step(
            p, own_wave, lane_scales, mixers, wide, tall, fourier, spectral, updated
        )
        rest(p, *there[p][:4]).wait_send()
        first, count = PHASES[p]
        for t in range(first, first + count):
            scatter_tiles(t, fourier, send)
        launch(p, *back[p])
    for phase in range(3):
        arrive(phase, *back[phase])
        first, count = PHASES[phase]
        for t in range(first, first + count):
            open_tiles(t, returned, chunks)
    for f in range(3):
        synthesise(f, chunks, table, y, columns, grid)
        pltpu.make_async_copy(field_of(grid, f), field_of(out_hbm, f), out_sem.at[f]).start()
    for f in range(3):
        pltpu.make_async_copy(field_of(grid, f), field_of(out_hbm, f), out_sem.at[f]).wait()
    for phase in range(3):
        rest(phase, *back[phase][:4]).wait_send()


def step(*inputs):
    vmem = pl.BlockSpec(memory_space=pltpu.VMEM)
    smem = pl.BlockSpec(memory_space=pltpu.SMEM)
    hbm = pl.BlockSpec(memory_space=pl.ANY)
    block = (128, 7, 16, 128)
    scratch = [
        ((1152, POINTS), BF16),
        ((3, WIDTH + 1, NLAT), BF16),
        ((3, POINTS, 512), BF16),
        ((128, 512), F32),
        ((128, 512), F32),
        ((24, 512), F32),
        ((24, 512), F32),
        ((12, 384, 128), F32),
        ((384, 1536), BF16),
        ((28, 32, 16, 128), BF16),
        (block, BF16),
        (block, BF16),
        (block, BF16),
        ((3, ROWS, 1536), BF16),
        ((3, 1536, DEPTH), BF16),
        ((3, 1536, 384), BF16),
        ((ROWS, 384), F32),
        ((DEPTH, 384), BF16),
        ((3, 256, 256), BF16),
    ]
    dma = pltpu.SemaphoreType.DMA
    return pl.pallas_call(
        step_kernel,
        out_shape=jax.ShapeDtypeStruct((1152, POINTS), BF16),
        in_specs=[hbm, hbm, vmem, vmem, vmem, vmem, vmem, smem, vmem, vmem],
        out_specs=hbm,
        scratch_shapes=[pltpu.VMEM(s, d) for s, d in scratch]
        + [dma((3,)), dma, dma((3,)), dma((6,)), dma((6,)), dma((6,))],
        compiler_params=pltpu.CompilerParams(
            vmem_limit_bytes=67043328, collective_id=0, has_side_effects=True
        ),
    )(*inputs)


def shards(
    grid,
    legendre,
    gauss_weights,
    band_counts,
    pair_m,
    vert_modes,
    mode_depth,
    diffusion,
    pressure_balance_matrix,
):
    lev_groups = 4
    fields, lat_cap, lev_dev, points = grid.shape
    my_band = lax.axis_index("lat")
    owner = my_band * lev_groups + lax.axis_index("lev")
    band_starts = jnp.cumsum(band_counts) - band_counts
    offsets = jnp.arange(lat_cap, dtype=jnp.int32)
    slot = jnp.where(
        offsets[None, :] < band_counts[:, None], band_starts[:, None] + offsets[None, :], -1
    ).astype(jnp.int32)
    my_start = lax.dynamic_slice(band_starts, (my_band,), (1,))[0]
    my_count = lax.dynamic_slice(band_counts, (my_band,), (1,))[0]
    padded = jnp.concatenate([gauss_weights, jnp.zeros((lat_cap,), F32)])
    weight = lax.dynamic_slice(padded, (my_start,), (lat_cap,)) * (1.0 / POINTS)
    weight = jnp.where(offsets < my_count, weight, 0.0)
    weight = jnp.broadcast_to(weight[:, None, None], (lat_cap, lev_dev, 128)).reshape(384, 128)

    lower = pair_m.reshape(4, 8, 4, 3).transpose(3, 0, 2, 1)
    waves = jnp.stack([lower, WIDTH - 1 - lower], axis=3)
    waves = jnp.broadcast_to(waves[:, :, :, :, None, :], (3, 4, 4, 2, 2, 8))
    part = jnp.broadcast_to(
        jnp.arange(2, dtype=jnp.int32)[None, None, None, None, :, None], waves.shape
    ).reshape(3, 1, 512)
    waves = waves.reshape(3, 1, 512).astype(F32)
    own_wave = lax.dynamic_slice(pair_m, (owner * 3,), (3,))

    def over_lanes(v):
        v = v.reshape(4, 1, 8)
        return jnp.broadcast_to(v, (4, 4, 8)).reshape(128)

    def mix(m):
        m = m.reshape(4, 1, 8, 4, 1, 8) * jnp.eye(4, dtype=F32).reshape(1, 4, 1, 1, 4, 1)
        return m.reshape(128, 128)

    lane_scales = jnp.stack([over_lanes(diffusion), over_lanes(mode_depth)])
    mixes = jnp.stack([mix(vert_modes.T), mix(vert_modes), mix(pressure_balance_matrix.T)])

    out = step(
        grid.reshape(1152, points),
        legendre,
        waves,
        part,
        weight,
        slot.reshape(1, 1536),
        slot.reshape(1536, 1),
        own_wave,
        lane_scales,
        mixes,
    )
    return out.reshape(fields, lat_cap, lev_dev, points)


def solution(mesh):
    placed = (
        P(None, "lat", "lev", None),
        P(("lat", "lev"), None, None),
        P(),
        P(),
        P(),
        P(),
        P(),
        P(),
        P(),
    )
    return jax.shard_map(
        shards, mesh=mesh, in_specs=placed, out_specs=P(None, "lat", "lev", None), check_vma=False
    )
```

time: 394 us -> 186 us (0.47)
  Pallas kernels: 271 us -> 155 us
  blocking collectives: 52.5 us -> 0 us
  waiting for transfers between devices: 37.6 us -> 0 us
  starting transfers between devices: 12.1 us -> 0 us
  local copies, waits for them, and re-layouts: 13.7 us -> 23.1 us
    pallas_call x3 -> x1, Pallas kernels: 271 us -> 155 us  [step(): pl.pallas_call(step_kernel, out_shape=jax.ShapeDtypeStruct((1152, POINTS)...]
    all_to_all x1 -> x0, blocking collectives: 52.5 us -> none  [shards(): received = lax.all_to_all(send, ('lat', 'lev'), 0, 0, tiled=True)]
    all_to_all x1 -> x0, waiting for transfers between devices: 37.6 us -> none  [shards(): received = lax.all_to_all(send, ('lat', 'lev'), 0, 0, tiled=True)]
    all_to_all x1 -> x0, starting transfers between devices: 12.1 us -> none  [shards(): received = lax.all_to_all(send, ('lat', 'lev'), 0, 0, tiled=True)]
    unnamed x10 -> x1, local copies, waits for them, and re-layouts: 0.02 us -> 6.03 us
  transfers between devices with their start and end apart: 1 -> 0, of which waited for: 1 -> 0; matrix products, arithmetic and copies ran while one was open for 2% -> 0% of each run, Pallas kernels for 0% -> 0%
where the time goes in v3:
time: 186 us; the launch traced here: 185 us
  Pallas kernels  155 us (83%)
  local copies, waits for them, and re-layouts  23.1 us (12%)
  other arithmetic  5.12 us (3%)
  between operations  2.06 us (1%)
    pallas_call x1, Pallas kernels, step(): pl.pallas_call(step_kernel, out_shape=jax.ShapeDtypeStruct((1152, POINTS)...  155 us
    unnamed x1, local copies, waits for them, and re-layouts  6.03 us
    mul x8, local copies, waits for them, and re-layouts, mix(): m.reshape(4, 1, 8, 4, 1, 8)  5.77 us

profile of v3, /device:TPU:1, one launch (start us, length us, event | category | flops | bytes accessed | tf_op | source)
XLA Modules:
  0.0 185.2 jit_solution(14345348232915206193)
XLA Ops:
  0.0 1.3 dynamic_slice.12
  1.3 1.3 dynamic_slice.15.own_wave
  2.6 0.7 broadcast_in_dim.64
  3.3 0.7 broadcast_in_dim.62
  4.8 0.7 copy.22
  5.7 0.7 sub.11
  8.9 1.5 compare_select_fusion
  10.4 0.7 add_select_fusion
  11.1 0.7 select_n.42.slot_row
  12.1 0.6 broadcast_in_dim.56.part
  12.7 0.9 reshape.245
  14.1 0.8 convert_element_type.19.wave
  14.9 0.8 mul.100
  15.8 0.8 mul.91
  16.7 0.8 mul.96
  17.5 0.8 broadcast_in_dim.60.weight
  18.3 1.3 select_n.45.slot_column
  19.6 0.8 broadcast_multiply_fusion.2
  20.4 1.0 mul.95
  21.5 1.0 mul.99
  22.5 1.0 mul.103
  23.6 0.7 pad_maximum_fusion.mixes
  24.2 154.9 %shard_map.91 = bf16[1152,2816]{1,0:T(8,128)(2,1)} custom-call(bf16[1152,2816]{1,0:T(8,128)(2,1)} %bitcast.20, bf16[3,769,1280]{2,1,0:T(8,128)(2,1)} %legendre_hbm.1, f32[3,1,512]{2,1,0:T(1,128)} %convert_element_type.19.wave, s32[3,1,512]{2,1,0:T(1,128)} %broadcast_in_dim.56.part, f32[384,128]{1,0:T(8,128)} %broadcast_in_dim.60.weight, ...), custom_call_target="tpu_custom_call" | custom-call | tf_op jit(solution)/shard_map/pallas_call | solution.py:443
  179.2 6.0 %copy.27 = bf16[3,48,8,2816]{3,2,1,0:T(8,128)(2,1)} copy(bf16[3,48,8,2816]{3,2,1,0:T(8,128)(2,1)} %bitcast.19) | data formatting | bytes 12976128
  (21 shorter events, 2.4 us)

commit v4 on v3

v4 whole, which is shorter than its diff:
```python
import math

import jax
import jax.numpy as jnp
from jax import lax
from jax.experimental import pallas as pl
from jax.experimental.pallas import tpu as pltpu
from jax.sharding import PartitionSpec as P

WIDTH = 768
NLAT = 1280
POINTS = 2816
ROWS = 784
DEPTH = 896
BANDS = 32
F32, BF16 = jnp.float32, jnp.bfloat16

WINDOWS = ((0, 384), (128, 640), (512, 640), (896, 384))


def swap(a, b, bit, low):
    return (
        jnp.where(low, a, pltpu.roll(b, bit, 1)),
        jnp.where(low, pltpu.roll(a, 128 - bit, 1), b),
    )


def exchange_bits(arrays, base, lane):
    arrays = list(arrays)
    step = 1
    while step < len(arrays):
        bit = base * step
        low = (lane & bit) == 0
        for i in range(len(arrays)):
            if not i & step:
                arrays[i], arrays[i | step] = swap(arrays[i], arrays[i | step], bit, low)
        step *= 2
    return arrays


def each(total, together, load, base, store):
    lane = lanes_of()

    def body(i, carry):
        groups = [load(i * together + u) for u in range(together)]
        groups = [exchange_bits(parts, base, lane) for parts in groups]
        for u, parts in enumerate(groups):
            store(i * together + u, parts)
        return carry

    lax.fori_loop(0, total // together, body, 0)


def lanes_of(rows=16):
    return lax.broadcasted_iota(jnp.int32, (rows, 128), 1)


def cos_sin(value, turn):
    quarter = POINTS // 4
    index = jnp.floor(value * (1.0 / quarter) + 0.5)
    angle = (value - index * quarter) * (2.0 * math.pi / POINTS)
    sq = angle * angle
    c = 1.0 + sq * (-0.5 + sq * (1 / 24 + sq * (-1 / 720 + sq * (1 / 40320))))
    s = angle * (1.0 + sq * (-1 / 6 + sq * (1 / 120 + sq * (-1 / 5040))))
    index = (index.astype(jnp.int32) + turn) & 3
    odd = (index & 1) == 1
    cos = jnp.where(odd, s, c)
    sin = jnp.where(odd, c, s)
    cos = jnp.where((index == 1) | (index == 2), -cos, cos)
    sin = jnp.where(index >= 2, -sin, sin)
    return cos, sin


def make_table(p, pairs, table, wave, b_cos, b_sin, a_cos, a_sin):
    lane = lax.broadcasted_iota(jnp.int32, (128, 128), 1)
    device = lax.broadcasted_iota(jnp.int32, (128, 128), 0)
    lower = pairs[:, p : p + 1].astype(F32)
    upper = (lanes_of(1) & 16) != 0
    for tile in range(4):
        chosen = device == 32 * tile + 4 * (lane & 7) + (lane >> 5)
        low = jnp.sum(jnp.where(chosen, lower, 0.0), axis=0, keepdims=True)
        wave[:, tile * 128 : tile * 128 + 128] = jnp.where(upper, WIDTH - 1 - low, low)
    w = wave[...]
    row = lax.broadcasted_iota(jnp.int32, (128, 512), 0).astype(F32)
    b_cos[...], b_sin[...] = cos_sin(row * w, 0)
    row = lax.broadcasted_iota(jnp.int32, (24, 512), 0).astype(F32)
    part = (lax.broadcasted_iota(jnp.int32, (24, 512), 1) >> 3) & 1
    a_cos[...], a_sin[...] = cos_sin(row * (128.0 * w), part)

    def fill(a, carry):
        values = a_cos[pl.ds(a, 1), :] * b_cos[...] - a_sin[pl.ds(a, 1), :] * b_sin[...]
        rows = pl.ds(pl.multiple_of(a * 128, 128), 128)
        table[rows, p * 512 : p * 512 + 512] = values.astype(BF16)
        return carry

    lax.fori_loop(0, POINTS // 128, fill, 0)


def analyse(p, grid, weight, table, y, chunks):
    def field(f, carry):
        base = pl.multiple_of(f * 384, 384)
        values = jnp.dot(
            grid[pl.ds(base, 384), :],
            table[:, p * 512 : p * 512 + 512],
            preferred_element_type=F32,
        )
        for tile in range(4):
            y[tile] = values[:, tile * 128 : tile * 128 + 128] * weight[...]

        def load(n):
            third, tile = n // 4, lax.rem(n, 4)
            return [
                y[tile, pl.ds(third * 128 + l, 16, stride=8), :].astype(BF16) for l in range(8)
            ]

        def store(n, parts):
            third, tile = n // 4, lax.rem(n, 4)
            for e, out in enumerate(parts):
                chunks[9 * p + 3 * f + third, tile * 8 + e] = out

        each(12, 4, load, 1, store)
        return carry

    lax.fori_loop(0, 3, field, 0)


def crossed(parts, cross):
    whole = jnp.concatenate([part.reshape(512, 128) for part in parts], axis=1)
    out = jnp.dot(whole, cross[...], preferred_element_type=F32).astype(BF16)
    return [out[:, i * 128 : i * 128 + 128].reshape(32, 16, 128) for i in range(4)]


def fours(i):
    return pl.ds(32 * i, 32)


def pack_chunks(t, chunks, cross, send):
    for x, out in enumerate(crossed([chunks[4 * t + g] for g in range(4)], cross)):
        send[fours(x), t] = out


def make_cross(cross):
    source = lax.broadcasted_iota(jnp.int32, (512, 512), 0)
    target = lax.broadcasted_iota(jnp.int32, (512, 512), 1)
    from_lane = ((source >> 5) & 3) * 128 + (source >> 7) * 32 + (source & 31)
    cross[...] = jnp.where(from_lane == target, 1.0, 0.0).astype(BF16)


def spread_legendre(p, legendre, slot_row, slot_column, wide, tall):
    wide[p * ROWS + 768 : p * ROWS + ROWS, :] = jnp.zeros((16, 1536), BF16)
    tall[p, :, 768:DEPTH] = jnp.zeros((1536, 128), BF16)
    for tile, (low, size) in enumerate(WINDOWS):
        at = tile * 384
        part = legendre[p, :, low : low + size]
        row = lax.broadcasted_iota(jnp.int32, (size, 384), 0) + low
        pick = jnp.where(row == slot_row[:, at : at + 384], 1.0, 0.0).astype(BF16)
        wide[p * ROWS : p * ROWS + WIDTH + 1, at : at + 384] = jnp.dot(
            part, pick, preferred_element_type=F32
        ).astype(BF16)
        row = lax.broadcasted_iota(jnp.int32, (384, size), 1) + low
        pick = jnp.where(row == slot_column[at : at + 384, :], 1.0, 0.0).astype(BF16)
        tall[p, at : at + 384, 0 : WIDTH + 1] = lax.dot_general(
            pick, part, (((1,), (1,)), ((), ())), preferred_element_type=F32
        ).astype(BF16)


def gather_tiles(t, received, cross, fourier):
    for g, out in enumerate(crossed([received[fours(v), t] for v in range(4)], cross)):
        q = 4 * t + g
        if q < 27:
            f, third = q % 9 // 3, q % 3
            fourier[q // 9, :, third, :, f * 128 : f * 128 + 128] = out


def mixed(values, mixer):
    high = values.astype(BF16)
    low = (values - high.astype(F32)).astype(BF16)
    out = jnp.dot(
        jnp.concatenate([high, low], axis=1), mixer, preferred_element_type=F32
    )
    return out[:, 0:128] + out[:, 128:256]


def spectral_step(p, wave, lane_scales, mixers, wide, tall, fourier, spectral, updated):
    spectral[...] = jnp.dot(
        wide[p * ROWS : p * ROWS + ROWS, :],
        fourier[p].reshape(1536, 384),
        preferred_element_type=F32,
    )
    updated[ROWS:DEPTH, :] = jnp.zeros((DEPTH - ROWS, 384), BF16)
    for at, size in ((0, 400), (400, 384)):
        k = lax.broadcasted_iota(jnp.int32, (size, 128), 0) + at
        own = k < WIDTH - wave
        degree = jnp.where(own, wave + k, k - 1)
        ratio = (degree * (degree + 1)).astype(F32) * (1.0 / float(WIDTH * (WIDTH - 1)))
        keep = (own != ((lanes_of(size) & 16) != 0)) & (k <= WIDTH)
        rows = slice(at, at + size)
        first = spectral[rows, 0:128] / (1.0 + lane_scales[0:1, :] * ratio * ratio)
        modes = mixed(spectral[rows, 128:256], mixers[0])
        modes = modes / (1.0 + lane_scales[1:2, :] * ratio)
        second = mixed(modes, mixers[1])
        third = spectral[rows, 256:384] - mixed(second, mixers[2])
        for f, values in enumerate((first, second, third)):
            updated[rows, f * 128 : f * 128 + 128] = jnp.where(keep, values, 0.0).astype(BF16)
    double = (lax.broadcasted_iota(jnp.int32, (1, 384), 1) & 16 != 0) | (wave > 0)
    factor = jnp.where(double, 2.0, 1.0)

    def rows_of(i, carry):
        at = pl.multiple_of(i * 384, 384)
        values = jnp.dot(tall[p, pl.ds(at, 384), :], updated[...], preferred_element_type=F32)
        out = (values * factor).astype(BF16)
        fourier[p, pl.ds(pl.multiple_of(i * 8, 8), 8)] = out.reshape(8, 3, 16, 384)
        return carry

    lax.fori_loop(0, 4, rows_of, 0)


def scatter_tiles(t, synthesis, cross, send):
    parts = []
    for q in range(4 * t, 4 * t + 4):
        q = min(q, 26)
        f, third = q % 9 // 3, q % 3
        parts.append(synthesis[q // 9, :, third, :, f * 128 : f * 128 + 128])
    for v, out in enumerate(crossed(parts, cross)):
        send[fours(v), t] = out


def open_tiles(t, received, cross, chunks):
    for g, out in enumerate(crossed([received[fours(x), t] for x in range(4)], cross)):
        if 4 * t + g < 27:
            chunks[4 * t + g] = out


def arrange(p, f, chunks, y, columns):
    def load(n):
        third, tile = n // 4, lax.rem(n, 4)
        return [chunks[9 * p + 3 * f + third, tile * 8 + e] for e in range(8)]

    def store(n, parts):
        third, tile = n // 4, lax.rem(n, 4)
        for l, values in enumerate(parts):
            y[tile, pl.ds(third * 128 + l, 16, stride=8), :] = values.astype(F32)

    each(12, 4, load, 1, store)
    for tile in range(4):
        at = p * 512 + tile * 128
        columns[f * 384 : f * 384 + 384, at : at + 128] = y[tile].astype(BF16)


def synthesise(i, columns, table, out):
    at = pl.multiple_of(i * 256, 256)
    out[:, pl.ds(at, 256)] = lax.dot_general(
        columns[...],
        table[pl.ds(at, 256), :],
        (((1,), (1,)), ((), ())),
        preferred_element_type=F32,
    ).astype(BF16)


def prepare(band_counts, gauss, weight, slot_row, slot_column):
    lat = lax.axis_index("lat")
    place_ = lax.broadcasted_iota(jnp.int32, (1, 1536), 1)
    offset = lax.broadcasted_iota(jnp.int32, (48, 1), 0)
    row = jnp.full((1, 1536), -1, jnp.int32)
    start, mine, count = 0, 0, 0
    for b in range(BANDS):
        size = band_counts[b]
        inside = place_ - 48 * b
        row = jnp.where((inside >= 0) & (inside < size), start + inside, row)
        slot_column[48 * b : 48 * b + 48, :] = jnp.where(offset < size, start + offset, -1)
        mine = mine + jnp.where(b < lat, size, 0)
        count = count + jnp.where(b == lat, size, 0)
        start = start + size
    slot_row[...] = row
    wanted = jnp.where(offset < count, mine + offset, -1)
    column = lax.broadcasted_iota(jnp.int32, (48, NLAT), 1)
    chosen = jnp.where(column == wanted, gauss[...], 0.0)
    values = jnp.sum(chosen, axis=1, keepdims=True) * (1.0 / POINTS)
    for r in range(48):
        weight[8 * r : 8 * r + 8, :] = jnp.broadcast_to(values[r : r + 1, :], (8, 128))


def over_lanes(row, spread):
    return lax.dot_general(
        row,
        spread,
        (((1,), (1,)), ((), ())),
        precision=lax.Precision.HIGHEST,
        preferred_element_type=F32,
    )


def make_mixers(vert_modes, mode_depth, diffusion, balance, lane_scales, mixers):
    lane = lax.broadcasted_iota(jnp.int32, (128, 32), 0)
    level = lax.broadcasted_iota(jnp.int32, (128, 32), 1)
    spread = jnp.where((lane >> 5) * 8 + (lane & 7) == level, 1.0, 0.0)
    lane_scales[0:1, :] = over_lanes(diffusion[...], spread)
    lane_scales[1:2, :] = over_lanes(mode_depth[...], spread)
    spread = spread.astype(BF16)
    one = (lax.broadcasted_iota(jnp.int32, (128, 128), 0) >> 3) & 3
    two = (lax.broadcasted_iota(jnp.int32, (128, 128), 1) >> 3) & 3

    def widen(m, side):
        half = lax.dot_general(
            spread, m, (((1,), (side,)), ((), ())), preferred_element_type=F32
        ).astype(BF16)
        full = lax.dot_general(
            half, spread, (((1,), (1,)), ((), ())), preferred_element_type=F32
        )
        return jnp.where(one == two, full, 0.0).astype(BF16)

    for i, (m, side) in enumerate(((vert_modes, 1), (vert_modes, 0), (balance, 1))):
        high = m[...].astype(BF16)
        low = (m[...] - high.astype(F32)).astype(BF16)
        wide_high = widen(high, side)
        mixers[i, 0:128, 0:128] = wide_high
        mixers[i, 128:256, 0:128] = wide_high
        mixers[i, 0:128, 128:256] = widen(low, side)
        mixers[i, 128:256, 128:256] = jnp.zeros((128, 128), BF16)


PHASES = ((0, 2), (2, 2), (4, 3))


def place():
    lat, lev = lax.axis_index("lat"), lax.axis_index("lev")
    return lat, lev, lev * 32 + lat


def partners():
    lat, lev, _ = place()
    zs = [lax.rem(lat // 8 + i, 4) * 8 for i in range(4)]
    ys = [lax.rem(lat // 2 + i, 4) * 2 for i in range(4)]
    cores = [lax.rem(lat + i, 2) for i in range(2)]
    levs = [lax.rem(lev + i, 4) for i in range(4)]
    for k in range(1, 128):
        step = k * 37 % 128
        yield zs[step // 32] + ys[step // 8 % 4] + cores[step % 2], levs[step // 2 % 4]


def greet_all():
    barrier = pltpu.get_barrier_semaphore()
    for to in partners():
        pl.semaphore_signal(
            barrier, inc=1, device_id=to, device_id_type=pl.DeviceIdType.MESH
        )


def hear_all():
    pl.semaphore_wait(pltpu.get_barrier_semaphore(), 127)


def launch(phase, send, received, send_sem, recv_sem, own_sem):
    _, _, me = place()
    first, count = PHASES[phase]
    tiles = pl.ds(first, count)
    pltpu.make_async_copy(send.at[me, tiles], received.at[me, tiles], own_sem).start()
    for to in partners():
        pltpu.make_async_remote_copy(
            src_ref=send.at[to[1] * 32 + to[0], tiles],
            dst_ref=received.at[me, tiles],
            send_sem=send_sem,
            recv_sem=recv_sem,
            device_id=to,
            device_id_type=pl.DeviceIdType.MESH,
        ).start()


def rest(phase, send, received, send_sem, recv_sem):
    lat, lev, _ = place()
    first, count = PHASES[phase]
    others = pl.ds(0, 127), pl.ds(first, count)
    return pltpu.make_async_remote_copy(
        src_ref=send.at[others],
        dst_ref=received.at[others],
        send_sem=send_sem,
        recv_sem=recv_sem,
        device_id=(lat, lev),
        device_id_type=pl.DeviceIdType.MESH,
    )


def arrive(phase, send, received, send_sem, recv_sem, own_sem):
    _, _, me = place()
    first, count = PHASES[phase]
    tiles = pl.ds(first, count)
    pltpu.make_async_copy(send.at[me, tiles], received.at[me, tiles], own_sem).wait()
    rest(phase, send, received, send_sem, recv_sem).wait_recv()


def wait_sent(phase, send, received, send_sem, recv_sem, own_sem):
    rest(phase, send, received, send_sem, recv_sem).wait_send()


def tiles_of(phase):
    first, count = PHASES[phase]
    return range(first, first + count)


def step_kernel(
    grid_hbm, legendre_hbm, pairs, pair_m, band_counts, gauss, vert_modes, mode_depth, diffusion,
    balance, out_hbm,
    grid, legendre, table, wave, b_cos, b_sin, a_cos, a_sin, y, chunks,
    send, received, returned, wide, tall, fourier, spectral, updated, mixers, cross,
    weight, slot_row, slot_column, lane_scales,
    grid_sem, legendre_sem, out_sem, send_sem, recv_sem, own_sem,
):
    def field_of(ref, f):
        return ref.at[pl.ds(f * 384, 384)]

    for f in range(3):
        pltpu.make_async_copy(field_of(grid_hbm, f), field_of(grid, f), grid_sem.at[f]).start()
    pltpu.make_async_copy(legendre_hbm, legendre, legendre_sem).start()
    greet_all()
    chunks[27] = jnp.zeros(chunks.shape[1:], BF16)
    there = [
        (send, received, send_sem.at[i], recv_sem.at[i], own_sem.at[i]) for i in range(3)
    ]
    back = [
        (send, returned, send_sem.at[3 + i], recv_sem.at[3 + i], own_sem.at[3 + i])
        for i in range(3)
    ]
    make_cross(cross)
    prepare(band_counts, gauss, weight, slot_row, slot_column)
    for p in range(3):
        make_table(p, pairs, table, wave, b_cos, b_sin, a_cos, a_sin)
        if p == 0:
            for f in range(3):
                pltpu.make_async_copy(
                    field_of(grid_hbm, f), field_of(grid, f), grid_sem.at[f]
                ).wait()
        analyse(p, grid, weight, table, y, chunks)
        for t in tiles_of(p):
            pack_chunks(t, chunks, cross, send)
        if p == 0:
            hear_all()
        launch(p, *there[p])
    pltpu.make_async_copy(legendre_hbm, legendre, legendre_sem).wait()
    make_mixers(vert_modes, mode_depth, diffusion, balance, lane_scales, mixers)
    lat, lev, _ = place()
    spread_legendre(0, legendre, slot_row, slot_column, wide, tall)
    for p in range(3):
        for phase in ((0, 1), (2,), ())[p]:
            arrive(phase, *there[phase])
            for t in tiles_of(phase):
                gather_tiles(t, received, cross, fourier)
        spectral_step(
            p, pair_m[3 * (4 * lat + lev) + p], lane_scales, mixers, wide, tall, fourier, spectral, updated
        )
        wait_sent(p, *there[p])
        for t in tiles_of(p):
            scatter_tiles(t, fourier, cross, send)
        launch(p, *back[p])
        if p == 0:
            for other in (1, 2):
                spread_legendre(other, legendre, slot_row, slot_column, wide, tall)
    columns = wide.at[0:1152]
    done = 0
    for phase in range(3):
        arrive(phase, *back[phase])
        for t in tiles_of(phase):
            open_tiles(t, returned, cross, chunks)
        ready = min(4 * (tiles_of(phase)[-1] + 1), 27) // 3
        for unit in range(done, ready):
            arrange(unit // 3, unit % 3, chunks, y, columns)
        done = ready

    def part_of(ref, i):
        return ref.at[:, pl.ds(pl.multiple_of(i * 256, 256), 256)]

    def points(i, carry):
        synthesise(i, columns, table, grid)
        pltpu.make_async_copy(part_of(grid, i), part_of(out_hbm, i), out_sem).start()
        return carry

    lax.fori_loop(0, POINTS // 256, points, 0)
    pltpu.make_async_copy(grid, out_hbm, out_sem).wait()
    for phase in range(3):
        wait_sent(phase, *back[phase])


def step(*inputs):
    vmem = pl.BlockSpec(memory_space=pltpu.VMEM)
    smem = pl.BlockSpec(memory_space=pltpu.SMEM)
    hbm = pl.BlockSpec(memory_space=pl.ANY)
    block = (128, 7, 16, 128)
    scratch = [
        ((1152, POINTS), BF16),
        ((3, WIDTH + 1, NLAT), BF16),
        ((POINTS, 1536), BF16),
        ((1, 512), F32),
        ((128, 512), F32),
        ((128, 512), F32),
        ((24, 512), F32),
        ((24, 512), F32),
        ((4, 384, 128), F32),
        ((28, 32, 16, 128), BF16),
        (block, BF16),
        (block, BF16),
        (block, BF16),
        ((3 * ROWS, 1536), BF16),
        ((3, 1536, DEPTH), BF16),
        ((3, 32, 3, 16, 384), BF16),
        ((ROWS, 384), F32),
        ((DEPTH, 384), BF16),
        ((3, 256, 256), BF16),
        ((512, 512), BF16),
        ((384, 128), F32),
        ((1, 1536), jnp.int32),
        ((1536, 1), jnp.int32),
        ((2, 128), F32),
    ]
    dma = pltpu.SemaphoreType.DMA
    return pl.pallas_call(
        step_kernel,
        out_shape=jax.ShapeDtypeStruct((1152, POINTS), BF16),
        in_specs=[hbm, hbm, vmem, smem, smem] + [vmem] * 5,
        out_specs=hbm,
        scratch_shapes=[pltpu.VMEM(s, d) for s, d in scratch]
        + [dma((3,)), dma, dma, dma((6,)), dma((6,)), dma((6,))],
        compiler_params=pltpu.CompilerParams(
            vmem_limit_bytes=67043328, collective_id=0, has_side_effects=True
        ),
    )(*inputs)


def shards(
    grid,
    legendre,
    gauss_weights,
    band_counts,
    pair_m,
    vert_modes,
    mode_depth,
    diffusion,
    pressure_balance_matrix,
):
    fields, lat_cap, lev_dev, points = grid.shape
    out = step(
        grid.reshape(fields * lat_cap * lev_dev, points),
        legendre,
        pair_m.reshape(128, 3),
        pair_m,
        band_counts,
        gauss_weights.reshape(1, NLAT),
        vert_modes,
        mode_depth.reshape(1, 32),
        diffusion.reshape(1, 32),
        pressure_balance_matrix,
    )
    return out.reshape(fields, lat_cap, lev_dev, points)


def solution(mesh):
    placed = (
        P(None, "lat", "lev", None),
        P(("lat", "lev"), None, None),
        P(),
        P(),
        P(),
        P(),
        P(),
        P(),
        P(),
    )
    return jax.shard_map(
        shards, mesh=mesh, in_specs=placed, out_specs=P(None, "lat", "lev", None), check_vma=False
    )
```

time: 186 us -> 127 us (0.68)
  Pallas kernels: 155 us -> 118 us
  local copies, waits for them, and re-layouts: 23.1 us -> 8.84 us
  other arithmetic: 5.12 us -> 0 us
  between operations: 2.06 us -> 0.01 us
    pallas_call x1, Pallas kernels: 155 us -> 118 us  [step(): pl.pallas_call(step_kernel, out_shape=jax.ShapeDtypeStruct((1152, POINTS)...]
    mul x8 -> x0, local copies, waits for them, and re-layouts: 5.77 us -> none  [mix(): m.reshape(4, 1, 8, 4, 1, 8)]
    dynamic_slice x3 -> x0, local copies, waits for them, and re-layouts: 3.18 us -> none  [the longest x1 1.32 us: shards(): my_count = lax.dynamic_slice(band_counts, (my_band,), (1,))[0]]
    broadcast_in_dim x11 -> x0, local copies, waits for them, and re-layouts: 3.18 us -> none  [the longest x4 1.48 us: over_lanes(): return jnp.broadcast_to(v, (4, 4, 8)).reshape(128)]
    select_n x2 -> x0, other arithmetic: 2.19 us -> none  [the longest x1 1.47 us: shards(): weight = jnp.where(offsets < my_count, weight, 0.0)]
    select_n x2 -> x0, local copies, waits for them, and re-layouts: 1.95 us -> none  [shards(): jnp.where(offsets[None, :] < band_counts[:, None], band_starts[:, None] +...]
    reshape x1 -> x2, local copies, waits for them, and re-layouts: 0.93 us -> 2.81 us  [the longest x1 1.52 us: shards(): pair_m.reshape(128, 3)]
where the time goes in v4:
time: 127 us
  Pallas kernels  118 us (93%)
  local copies, waits for them, and re-layouts  8.84 us (7%)
    pallas_call x1, Pallas kernels, step(): pl.pallas_call(step_kernel, out_shape=jax.ShapeDtypeStruct((1152, POINTS)...  118 us
    unnamed x1, local copies, waits for them, and re-layouts  6.03 us

profile of v4, /device:TPU:1, one launch (start us, length us, event | category | flops | bytes accessed | tf_op | source)
XLA Modules:
  0.0 126.8 jit_solution(3530448478662874084)
XLA Ops:
  0.0 1.3 %reshape.20.gauss = f32[1,1280]{1,0:T(1,128)} reshape(f32[1280]{0:T(1024)} %param.11) | data formatting | bytes 10240 | tf_op jit(solution)/shard_map/reshape | solution.py:545
  1.3 1.5 %reshape.19.pairs = s32[128,3]{1,0:T(8,128)} reshape(s32[384]{0:T(512)} %pair_m.1) | data formatting | bytes 3072 | tf_op jit(solution)/shard_map/reshape | solution.py:542
  2.8 117.9 %shard_map.91 = bf16[1152,2816]{1,0:T(8,128)(2,1)} custom-call(bf16[1152,2816]{1,0:T(8,128)(2,1)} %bitcast.5, bf16[3,769,1280]{2,1,0:T(8,128)(2,1)} %legendre_hbm.1, s32[128,3]{1,0:T(8,128)} %reshape.19.pairs, s32[384]{0:T(512)} %pair_m.1, s32[32]{0:T(128)} %band_counts.1, f32[1,1280]{1,0:T(1,128)} %reshape.20.gauss, f32[32,32]{1,0:T(8,128)} %vert_modes.1, ...), custom_call_target="tpu_custom_call" | custom-call | tf_op jit(solution)/shard_map/pallas_call | solution.py:514
  120.8 6.0 %copy.11 = bf16[3,48,8,2816]{3,2,1,0:T(8,128)(2,1)} copy(bf16[3,48,8,2816]{3,2,1,0:T(8,128)(2,1)} %bitcast.4) | data formatting | bytes 12976128

commit v5 on v4

--- a/solution.py
+++ b/solution.py
@@ -74,7 +74,11 @@
 def make_table(p, pairs, table, wave, b_cos, b_sin, a_cos, a_sin):
     lane = lax.broadcasted_iota(jnp.int32, (128, 128), 1)
     device = lax.broadcasted_iota(jnp.int32, (128, 128), 0)
-    lower = pairs[:, p : p + 1].astype(F32)
+    lane384 = lax.broadcasted_iota(jnp.int32, (128, 384), 1)
+    device384 = lax.broadcasted_iota(jnp.int32, (128, 384), 0)
+    pair = pairs[...].reshape(1, 384).astype(F32)
+    lower = jnp.where(lane384 == 3 * device384 + p, pair, 0.0)
+    lower = jnp.sum(lower, axis=1, keepdims=True)
     upper = (lanes_of(1) & 16) != 0
     for tile in range(4):
         chosen = device == 32 * tile + 4 * (lane & 7) + (lane >> 5)
@@ -96,7 +100,7 @@
     lax.fori_loop(0, POINTS // 128, fill, 0)
 
 
-def analyse(p, grid, weight, table, y, chunks):
+def analyse(p, grid, weight, table, y, stage, turn, chunks):
     def field(f, carry):
         base = pl.multiple_of(f * 384, 384)
         values = jnp.dot(
@@ -107,21 +111,19 @@
         for tile in range(4):
             y[tile] = values[:, tile * 128 : tile * 128 + 128] * weight[...]
 
-        def load(n):
-            third, tile = n // 4, lax.rem(n, 4)
-            return [
-                y[tile, pl.ds(third * 128 + l, 16, stride=8), :].astype(BF16) for l in range(8)
-            ]
-
-        def store(n, parts):
-            third, tile = n // 4, lax.rem(n, 4)
-            for e, out in enumerate(parts):
-                chunks[9 * p + 3 * f + third, tile * 8 + e] = out
-
-        each(12, 4, load, 1, store)
+        for third in range(3):
+            for tile in range(4):
+                at = pl.multiple_of(f * 192 + (4 * third + tile) * 16, 16)
+                for l in range(8):
+                    stage[pl.ds(at, 16), l * 128 : l * 128 + 128] = y[
+                        tile, pl.ds(third * 128 + l, 16, stride=8), :
+                    ].astype(BF16)
         return carry
 
     lax.fori_loop(0, 3, field, 0)
+    chunks[p * 576 : p * 576 + 576, :] = jnp.dot(
+        stage[0:576, 0:1024], turn[...], preferred_element_type=F32
+    ).astype(BF16)
 
 
 def crossed(parts, cross):
@@ -135,8 +137,22 @@
 
 
 def pack_chunks(t, chunks, cross, send):
-    for x, out in enumerate(crossed([chunks[4 * t + g] for g in range(4)], cross)):
+    parts = []
+    for g in range(4):
+        rows = chunks[pl.ds(pl.multiple_of(t * 256 + g * 64, 64), 64), :]
+        parts.append(
+            jnp.concatenate([rows[:, e * 128 : e * 128 + 128] for e in range(8)], axis=0)
+        )
+    for x, out in enumerate(crossed(parts, cross)):
         send[fours(x), t] = out
+
+
+def make_turn(turn):
+    source = lax.broadcasted_iota(jnp.int32, (1024, 128), 0)
+    target = lax.broadcasted_iota(jnp.int32, (1024, 128), 1)
+    for e in range(8):
+        from_lane = (target & 7) * 128 + (target >> 3) * 8 + e
+        turn[:, e * 128 : e * 128 + 128] = jnp.where(source == from_lane, 1.0, 0.0).astype(BF16)
 
 
 def make_cross(cross):
@@ -147,14 +163,15 @@
 
 
 def spread_legendre(p, legendre, slot_row, slot_column, wide, tall):
-    wide[p * ROWS + 768 : p * ROWS + ROWS, :] = jnp.zeros((16, 1536), BF16)
+    base = p * ROWS if isinstance(p, int) else pl.multiple_of(p * ROWS, 16)
+    wide[pl.ds(base + 768, 16), :] = jnp.zeros((16, 1536), BF16)
     tall[p, :, 768:DEPTH] = jnp.zeros((1536, 128), BF16)
     for tile, (low, size) in enumerate(WINDOWS):
         at = tile * 384
         part = legendre[p, :, low : low + size]
         row = lax.broadcasted_iota(jnp.int32, (size, 384), 0) + low
         pick = jnp.where(row == slot_row[:, at : at + 384], 1.0, 0.0).astype(BF16)
-        wide[p * ROWS : p * ROWS + WIDTH + 1, at : at + 384] = jnp.dot(
+        wide[pl.ds(base, WIDTH + 1), at : at + 384] = jnp.dot(
             part, pick, preferred_element_type=F32
         ).astype(BF16)
         row = lax.broadcasted_iota(jnp.int32, (384, size), 1) + low
@@ -227,14 +244,17 @@
 
 def open_tiles(t, received, cross, chunks):
     for g, out in enumerate(crossed([received[fours(x), t] for x in range(4)], cross)):
-        if 4 * t + g < 27:
-            chunks[4 * t + g] = out
+        rows = pl.ds(pl.multiple_of(t * 256 + g * 64, 64), 64)
+        out = out.reshape(512, 128)
+        for e in range(8):
+            chunks[rows, e * 128 : e * 128 + 128] = out[e * 64 : e * 64 + 64]
 
 
 def arrange(p, f, chunks, y, columns):
     def load(n):
         third, tile = n // 4, lax.rem(n, 4)
-        return [chunks[9 * p + 3 * f + third, tile * 8 + e] for e in range(8)]
+        at = pl.multiple_of((9 * p + 3 * f + third) * 64 + tile * 16, 16)
+        return [chunks[pl.ds(at, 16), e * 128 : e * 128 + 128] for e in range(8)]
 
     def store(n, parts):
         third, tile = n // 4, lax.rem(n, 4)
@@ -247,37 +267,44 @@
         columns[f * 384 : f * 384 + 384, at : at + 128] = y[tile].astype(BF16)
 
 
-def synthesise(i, columns, table, out):
-    at = pl.multiple_of(i * 256, 256)
-    out[:, pl.ds(at, 256)] = lax.dot_general(
-        columns[...],
-        table[pl.ds(at, 256), :],
+def synthesise(i, rows, low, high, columns, table, out, add):
+    at = pl.ds(pl.multiple_of(i * 256, 256), 256)
+    values = lax.dot_general(
+        columns[rows, low:high],
+        table[at, low:high],
         (((1,), (1,)), ((), ())),
         preferred_element_type=F32,
-    ).astype(BF16)
-
-
-def prepare(band_counts, gauss, weight, slot_row, slot_column):
+    )
+    if add:
+        values = values + out[rows, at].astype(F32)
+    out[rows, at] = values.astype(BF16)
+
+
+def row_weights(band_counts, gauss, weight):
     lat = lax.axis_index("lat")
-    place_ = lax.broadcasted_iota(jnp.int32, (1, 1536), 1)
+    start, count = 0, 0
+    for b in range(BANDS):
+        size = band_counts[b]
+        start = start + jnp.where(b < lat, size, 0)
+        count = count + jnp.where(b == lat, size, 0)
+    for r in range(48):
+        value = gauss[jnp.minimum(start + r, NLAT - 1)] * (1.0 / POINTS)
+        value = jnp.where(r < count, value, 0.0)
+        weight[8 * r : 8 * r + 8, :] = jnp.broadcast_to(value, (8, 128))
+
+
+def slot_latitudes(band_counts, slot_row, slot_column):
+    slot = lax.broadcasted_iota(jnp.int32, (1, 1536), 1)
     offset = lax.broadcasted_iota(jnp.int32, (48, 1), 0)
     row = jnp.full((1, 1536), -1, jnp.int32)
-    start, mine, count = 0, 0, 0
+    start = 0
     for b in range(BANDS):
         size = band_counts[b]
-        inside = place_ - 48 * b
+        inside = slot - 48 * b
         row = jnp.where((inside >= 0) & (inside < size), start + inside, row)
         slot_column[48 * b : 48 * b + 48, :] = jnp.where(offset < size, start + offset, -1)
-        mine = mine + jnp.where(b < lat, size, 0)
-        count = count + jnp.where(b == lat, size, 0)
         start = start + size
     slot_row[...] = row
-    wanted = jnp.where(offset < count, mine + offset, -1)
-    column = lax.broadcasted_iota(jnp.int32, (48, NLAT), 1)
-    chosen = jnp.where(column == wanted, gauss[...], 0.0)
-    values = jnp.sum(chosen, axis=1, keepdims=True) * (1.0 / POINTS)
-    for r in range(48):
-        weight[8 * r : 8 * r + 8, :] = jnp.broadcast_to(values[r : r + 1, :], (8, 128))
 
 
 def over_lanes(row, spread):
@@ -324,23 +351,25 @@
 
 def place():
     lat, lev = lax.axis_index("lat"), lax.axis_index("lev")
-    return lat, lev, lev * 32 + lat
+    return lat, lev, lev * 32 + lat, lev * 32 + lax.rem(lat, 8) * 4 + lat // 8
 
 
 def partners():
-    lat, lev, _ = place()
-    zs = [lax.rem(lat // 8 + i, 4) * 8 for i in range(4)]
+    lat, lev, _, _ = place()
+    zs = [lax.rem(lat // 8 + i, 4) for i in range(4)]
     ys = [lax.rem(lat // 2 + i, 4) * 2 for i in range(4)]
     cores = [lax.rem(lat + i, 2) for i in range(2)]
     levs = [lax.rem(lev + i, 4) for i in range(4)]
     for k in range(1, 128):
         step = k * 37 % 128
-        yield zs[step // 32] + ys[step // 8 % 4] + cores[step % 2], levs[step // 2 % 4]
+        z, low = zs[step // 32], ys[step // 8 % 4] + cores[step % 2]
+        x = levs[step // 2 % 4]
+        yield (z * 8 + low, x), x * 32 + z * 8 + low, x * 32 + low * 4 + z
 
 
 def greet_all():
     barrier = pltpu.get_barrier_semaphore()
-    for to in partners():
+    for to, _, _ in partners():
         pl.semaphore_signal(
             barrier, inc=1, device_id=to, device_id_type=pl.DeviceIdType.MESH
         )
@@ -350,15 +379,23 @@
     pl.semaphore_wait(pltpu.get_barrier_semaphore(), 127)
 
 
-def launch(phase, send, received, send_sem, recv_sem, own_sem):
-    _, _, me = place()
+def own_copy(phase, home, send, received, own_sem):
+    _, _, plain, folded = place()
     first, count = PHASES[phase]
     tiles = pl.ds(first, count)
-    pltpu.make_async_copy(send.at[me, tiles], received.at[me, tiles], own_sem).start()
-    for to in partners():
+    source, target = (plain, folded) if home else (folded, plain)
+    return pltpu.make_async_copy(send.at[source, tiles], received.at[target, tiles], own_sem)
+
+
+def launch(phase, home, send, received, send_sem, recv_sem, own_sem):
+    _, _, mine_plain, mine_folded = place()
+    first, count = PHASES[phase]
+    tiles = pl.ds(first, count)
+    own_copy(phase, home, send, received, own_sem).start()
+    for to, plain, folded in partners():
         pltpu.make_async_remote_copy(
-            src_ref=send.at[to[1] * 32 + to[0], tiles],
-            dst_ref=received.at[me, tiles],
+            src_ref=send.at[plain if home else folded, tiles],
+            dst_ref=received.at[mine_folded if home else mine_plain, tiles],
             send_sem=send_sem,
             recv_sem=recv_sem,
             device_id=to,
@@ -367,7 +404,7 @@
 
 
 def rest(phase, send, received, send_sem, recv_sem):
-    lat, lev, _ = place()
+    lat, lev, _, _ = place()
     first, count = PHASES[phase]
     others = pl.ds(0, 127), pl.ds(first, count)
     return pltpu.make_async_remote_copy(
@@ -380,15 +417,12 @@
     )
 
 
-def arrive(phase, send, received, send_sem, recv_sem, own_sem):
-    _, _, me = place()
-    first, count = PHASES[phase]
-    tiles = pl.ds(first, count)
-    pltpu.make_async_copy(send.at[me, tiles], received.at[me, tiles], own_sem).wait()
+def arrive(phase, home, send, received, send_sem, recv_sem, own_sem):
+    own_copy(phase, home, send, received, own_sem).wait()
     rest(phase, send, received, send_sem, recv_sem).wait_recv()
 
 
-def wait_sent(phase, send, received, send_sem, recv_sem, own_sem):
+def wait_sent(phase, home, send, received, send_sem, recv_sem, own_sem):
     rest(phase, send, received, send_sem, recv_sem).wait_send()
 
 
@@ -400,7 +434,7 @@
 def step_kernel(
     grid_hbm, legendre_hbm, pairs, pair_m, band_counts, gauss, vert_modes, mode_depth, diffusion,
     balance, out_hbm,
-    grid, legendre, table, wave, b_cos, b_sin, a_cos, a_sin, y, chunks,
+    grid, legendre, table, wave, b_cos, b_sin, a_cos, a_sin, y, chunks, turn,
     send, received, returned, wide, tall, fourier, spectral, updated, mixers, cross,
     weight, slot_row, slot_column, lane_scales,
     grid_sem, legendre_sem, out_sem, send_sem, recv_sem, own_sem,
@@ -412,16 +446,17 @@
         pltpu.make_async_copy(field_of(grid_hbm, f), field_of(grid, f), grid_sem.at[f]).start()
     pltpu.make_async_copy(legendre_hbm, legendre, legendre_sem).start()
     greet_all()
-    chunks[27] = jnp.zeros(chunks.shape[1:], BF16)
+    chunks[27 * 64 :, :] = jnp.zeros((64, 1024), BF16)
+    make_turn(turn)
     there = [
-        (send, received, send_sem.at[i], recv_sem.at[i], own_sem.at[i]) for i in range(3)
+        (False, send, received, send_sem.at[i], recv_sem.at[i], own_sem.at[i]) for i in range(3)
     ]
     back = [
-        (send, returned, send_sem.at[3 + i], recv_sem.at[3 + i], own_sem.at[3 + i])
+        (True, send, returned, send_sem.at[3 + i], recv_sem.at[3 + i], own_sem.at[3 + i])
         for i in range(3)
     ]
+    row_weights(band_counts, gauss, weight)
     make_cross(cross)
-    prepare(band_counts, gauss, weight, slot_row, slot_column)
     for p in range(3):
         make_table(p, pairs, table, wave, b_cos, b_sin, a_cos, a_sin)
         if p == 0:
@@ -429,15 +464,20 @@
                 pltpu.make_async_copy(
                     field_of(grid_hbm, f), field_of(grid, f), grid_sem.at[f]
                 ).wait()
-        analyse(p, grid, weight, table, y, chunks)
-        for t in tiles_of(p):
+        analyse(p, grid, weight, table, y, wide, turn, chunks)
+
+        def pack(t, carry):
             pack_chunks(t, chunks, cross, send)
+            return carry
+
+        lax.fori_loop(tiles_of(p)[0], tiles_of(p)[-1] + 1, pack, 0)
         if p == 0:
             hear_all()
         launch(p, *there[p])
     pltpu.make_async_copy(legendre_hbm, legendre, legendre_sem).wait()
+    slot_latitudes(band_counts, slot_row, slot_column)
     make_mixers(vert_modes, mode_depth, diffusion, balance, lane_scales, mixers)
-    lat, lev, _ = place()
+    lat, lev, _, _ = place()
     spread_legendre(0, legendre, slot_row, slot_column, wide, tall)
     for p in range(3):
         for phase in ((0, 1), (2,), ())[p]:
@@ -452,24 +492,42 @@
             scatter_tiles(t, fourier, cross, send)
         launch(p, *back[p])
         if p == 0:
-            for other in (1, 2):
+
+
+            def spread(other, carry):
                 spread_legendre(other, legendre, slot_row, slot_column, wide, tall)
+                return carry
+
+            lax.fori_loop(1, 3, spread, 0)
     columns = wide.at[0:1152]
     done = 0
     for phase in range(3):
         arrive(phase, *back[phase])
-        for t in tiles_of(phase):
+
+        def unpack(t, carry):
             open_tiles(t, returned, cross, chunks)
+            return carry
+
+        lax.fori_loop(tiles_of(phase)[0], tiles_of(phase)[-1] + 1, unpack, 0)
         ready = min(4 * (tiles_of(phase)[-1] + 1), 27) // 3
         for unit in range(done, ready):
             arrange(unit // 3, unit % 3, chunks, y, columns)
         done = ready
+        if phase == 1:
+
+            def early(i, carry):
+                synthesise(i, slice(0, 768), 0, 1024, columns, table, grid, False)
+                synthesise(i, slice(768, 1152), 0, 512, columns, table, grid, False)
+                return carry
+
+            lax.fori_loop(0, POINTS // 256, early, 0)
 
     def part_of(ref, i):
         return ref.at[:, pl.ds(pl.multiple_of(i * 256, 256), 256)]
 
     def points(i, carry):
-        synthesise(i, columns, table, grid)
+        synthesise(i, slice(0, 768), 1024, 1536, columns, table, grid, True)
+        synthesise(i, slice(768, 1152), 512, 1536, columns, table, grid, True)
         pltpu.make_async_copy(part_of(grid, i), part_of(out_hbm, i), out_sem).start()
         return carry
 
@@ -494,7 +552,8 @@
         ((24, 512), F32),
         ((24, 512), F32),
         ((4, 384, 128), F32),
-        ((28, 32, 16, 128), BF16),
+        ((28 * 64, 1024), BF16),
+        ((1024, 1024), BF16),
         (block, BF16),
         (block, BF16),
         (block, BF16),
@@ -514,7 +573,7 @@
     return pl.pallas_call(
         step_kernel,
         out_shape=jax.ShapeDtypeStruct((1152, POINTS), BF16),
-        in_specs=[hbm, hbm, vmem, smem, smem] + [vmem] * 5,
+        in_specs=[hbm, hbm, vmem, smem, smem, smem] + [vmem] * 4,
         out_specs=hbm,
         scratch_shapes=[pltpu.VMEM(s, d) for s, d in scratch]
         + [dma((3,)), dma, dma, dma((6,)), dma((6,)), dma((6,))],
@@ -539,10 +598,10 @@
     out = step(
         grid.reshape(fields * lat_cap * lev_dev, points),
         legendre,
-        pair_m.reshape(128, 3),
+        pair_m,
         pair_m,
         band_counts,
-        gauss_weights.reshape(1, NLAT),
+        gauss_weights,
         vert_modes,
         mode_depth.reshape(1, 32),
         diffusion.reshape(1, 32),

time: 127 us -> 119 us (0.937)
  Pallas kernels: 118 us -> 113 us
  local copies, waits for them, and re-layouts: 8.84 us -> 6.03 us
    pallas_call x1, Pallas kernels: 118 us -> 113 us  [step(): pl.pallas_call(step_kernel, out_shape=jax.ShapeDtypeStruct((1152, POINTS)...]
    reshape x2 -> x0, local copies, waits for them, and re-layouts: 2.81 us -> none  [the longest x1 1.52 us: shards(): pair_m.reshape(128, 3)]
where the time goes in v5:
time: 119 us
  Pallas kernels  113 us (95%)
  local copies, waits for them, and re-layouts  6.03 us (5%)
    pallas_call x1, Pallas kernels, step(): pl.pallas_call(step_kernel, out_shape=jax.ShapeDtypeStruct((1152, POINTS)...  113 us
    unnamed x1, local copies, waits for them, and re-layouts  6.03 us

profile of v5, /device:TPU:1, one launch (start us, length us, event | category | flops | bytes accessed | tf_op | source)
XLA Modules:
  0.0 119.3 jit_solution(14147932727386741862)
XLA Ops:
  0.0 113.2 %shard_map.91 = bf16[1152,2816]{1,0:T(8,128)(2,1)} custom-call(bf16[1152,2816]{1,0:T(8,128)(2,1)} %bitcast.5, bf16[3,769,1280]{2,1,0:T(8,128)(2,1)} %legendre_hbm.1, s32[384]{0:T(512)} %pair_m.1, s32[384]{0:T(512)} %pair_m.1, s32[32]{0:T(128)} %band_counts.1, f32[1280]{0:T(1024)} %gauss.1, f32[32,32]{1,0:T(8,128)} %vert_modes.1, f32[1,32]{1,0:T(1,128)} %bitcast.6, ...), custom_call_target="tpu_custom_call" | custom-call | tf_op jit(solution)/shard_map/pallas_call | solution.py:573
  113.2 6.0 %copy.11 = bf16[3,48,8,2816]{3,2,1,0:T(8,128)(2,1)} copy(bf16[3,48,8,2816]{3,2,1,0:T(8,128)(2,1)} %bitcast.4) | data formatting | bytes 12976128

commit v6 on v5

--- a/solution.py
+++ b/solution.py
@@ -15,7 +15,7 @@
 BANDS = 32
 F32, BF16 = jnp.float32, jnp.bfloat16
 
-WINDOWS = ((0, 384), (128, 640), (512, 640), (896, 384))
+WINDOWS = ((0, 256), (0, 512), (256, 512), (512, 512), (768, 512), (1024, 256))
 
 
 def swap(a, b, bit, low):
@@ -167,16 +167,16 @@
     wide[pl.ds(base + 768, 16), :] = jnp.zeros((16, 1536), BF16)
     tall[p, :, 768:DEPTH] = jnp.zeros((1536, 128), BF16)
     for tile, (low, size) in enumerate(WINDOWS):
-        at = tile * 384
+        at = slice(tile * 256, tile * 256 + 256)
         part = legendre[p, :, low : low + size]
-        row = lax.broadcasted_iota(jnp.int32, (size, 384), 0) + low
-        pick = jnp.where(row == slot_row[:, at : at + 384], 1.0, 0.0).astype(BF16)
-        wide[pl.ds(base, WIDTH + 1), at : at + 384] = jnp.dot(
+        row = lax.broadcasted_iota(jnp.int32, (size, 256), 0) + low
+        pick = jnp.where(row == slot_row[:, at], 1.0, 0.0).astype(BF16)
+        wide[pl.ds(base, WIDTH + 1), at] = jnp.dot(
             part, pick, preferred_element_type=F32
         ).astype(BF16)
-        row = lax.broadcasted_iota(jnp.int32, (384, size), 1) + low
-        pick = jnp.where(row == slot_column[at : at + 384, :], 1.0, 0.0).astype(BF16)
-        tall[p, at : at + 384, 0 : WIDTH + 1] = lax.dot_general(
+        row = lax.broadcasted_iota(jnp.int32, (256, size), 1) + low
+        pick = jnp.where(row == slot_column[at, :], 1.0, 0.0).astype(BF16)
+        tall[p, at, 0 : WIDTH + 1] = lax.dot_general(
             pick, part, (((1,), (1,)), ((), ())), preferred_element_type=F32
         ).astype(BF16)
 
@@ -347,6 +347,7 @@
 
 
 PHASES = ((0, 2), (2, 2), (4, 3))
+RETURNS = ((0, 2), (2, 2), (4, 2), (6, 1))
 
 
 def place():
@@ -381,16 +382,14 @@
 
 def own_copy(phase, home, send, received, own_sem):
     _, _, plain, folded = place()
-    first, count = PHASES[phase]
-    tiles = pl.ds(first, count)
+    tiles = pl.ds(*phase)
     source, target = (plain, folded) if home else (folded, plain)
     return pltpu.make_async_copy(send.at[source, tiles], received.at[target, tiles], own_sem)
 
 
 def launch(phase, home, send, received, send_sem, recv_sem, own_sem):
     _, _, mine_plain, mine_folded = place()
-    first, count = PHASES[phase]
-    tiles = pl.ds(first, count)
+    tiles = pl.ds(*phase)
     own_copy(phase, home, send, received, own_sem).start()
     for to, plain, folded in partners():
         pltpu.make_async_remote_copy(
@@ -405,8 +404,7 @@
 
 def rest(phase, send, received, send_sem, recv_sem):
     lat, lev, _, _ = place()
-    first, count = PHASES[phase]
-    others = pl.ds(0, 127), pl.ds(first, count)
+    others = pl.ds(0, 127), pl.ds(*phase)
     return pltpu.make_async_remote_copy(
         src_ref=send.at[others],
         dst_ref=received.at[others],
@@ -427,8 +425,7 @@
 
 
 def tiles_of(phase):
-    first, count = PHASES[phase]
-    return range(first, first + count)
+    return range(phase[0], phase[0] + phase[1])
 
 
 def step_kernel(
@@ -449,11 +446,12 @@
     chunks[27 * 64 :, :] = jnp.zeros((64, 1024), BF16)
     make_turn(turn)
     there = [
-        (False, send, received, send_sem.at[i], recv_sem.at[i], own_sem.at[i]) for i in range(3)
+        (PHASES[i], False, send, received, send_sem.at[i], recv_sem.at[i], own_sem.at[i])
+        for i in range(3)
     ]
     back = [
-        (True, send, returned, send_sem.at[3 + i], recv_sem.at[3 + i], own_sem.at[3 + i])
-        for i in range(3)
+        (RETURNS[i], True, send, returned, send_sem.at[3 + i], recv_sem.at[3 + i], own_sem.at[3 + i])
+        for i in range(4)
     ]
     row_weights(band_counts, gauss, weight)
     make_cross(cross)
@@ -470,10 +468,10 @@
             pack_chunks(t, chunks, cross, send)
             return carry
 
-        lax.fori_loop(tiles_of(p)[0], tiles_of(p)[-1] + 1, pack, 0)
+        lax.fori_loop(tiles_of(PHASES[p])[0], tiles_of(PHASES[p])[-1] + 1, pack, 0)
         if p == 0:
             hear_all()
-        launch(p, *there[p])
+        launch(*there[p])
     pltpu.make_async_copy(legendre_hbm, legendre, legendre_sem).wait()
     slot_latitudes(band_counts, slot_row, slot_column)
     make_mixers(vert_modes, mode_depth, diffusion, balance, lane_scales, mixers)
@@ -481,16 +479,17 @@
     spread_legendre(0, legendre, slot_row, slot_column, wide, tall)
     for p in range(3):
         for phase in ((0, 1), (2,), ())[p]:
-            arrive(phase, *there[phase])
-            for t in tiles_of(phase):
+            arrive(*there[phase])
+            for t in tiles_of(PHASES[phase]):
                 gather_tiles(t, received, cross, fourier)
         spectral_step(
             p, pair_m[3 * (4 * lat + lev) + p], lane_scales, mixers, wide, tall, fourier, spectral, updated
         )
-        wait_sent(p, *there[p])
-        for t in tiles_of(p):
-            scatter_tiles(t, fourier, cross, send)
-        launch(p, *back[p])
+        wait_sent(*there[p])
+        for i in ((0,), (1,), (2, 3))[p]:
+            for t in tiles_of(RETURNS[i]):
+                scatter_tiles(t, fourier, cross, send)
+            launch(*back[i])
         if p == 0:
 
 
@@ -500,41 +499,52 @@
 
             lax.fori_loop(1, 3, spread, 0)
     columns = wide.at[0:1152]
+    upper, lower = slice(0, 768), slice(768, 1152)
+
+    def each_part(work):
+        def body(i, carry):
+            work(i)
+            return carry
+
+        lax.fori_loop(0, POINTS // 256, body, 0)
+
+    def emit(i, rows, sem):
+        at = rows, pl.ds(pl.multiple_of(i * 256, 256), 256)
+        pltpu.make_async_copy(grid.at[at], out_hbm.at[at], sem).start()
+
+    def early(i):
+        synthesise(i, upper, 0, 1024, columns, table, grid, False)
+        synthesise(i, lower, 0, 512, columns, table, grid, False)
+
+    def middle(i):
+        synthesise(i, upper, 1024, 1536, columns, table, grid, True)
+        emit(i, upper, out_sem.at[0])
+        synthesise(i, lower, 512, 1024, columns, table, grid, True)
+
+    def late(i):
+        synthesise(i, lower, 1024, 1536, columns, table, grid, True)
+        emit(i, lower, out_sem.at[1])
+
     done = 0
-    for phase in range(3):
-        arrive(phase, *back[phase])
+    for i in range(4):
+        arrive(*back[i])
 
         def unpack(t, carry):
             open_tiles(t, returned, cross, chunks)
             return carry
 
-        lax.fori_loop(tiles_of(phase)[0], tiles_of(phase)[-1] + 1, unpack, 0)
-        ready = min(4 * (tiles_of(phase)[-1] + 1), 27) // 3
+        tiles = tiles_of(RETURNS[i])
+        lax.fori_loop(tiles[0], tiles[-1] + 1, unpack, 0)
+        ready = min(4 * (tiles[-1] + 1), 27) // 3
         for unit in range(done, ready):
             arrange(unit // 3, unit % 3, chunks, y, columns)
         done = ready
-        if phase == 1:
-
-            def early(i, carry):
-                synthesise(i, slice(0, 768), 0, 1024, columns, table, grid, False)
-                synthesise(i, slice(768, 1152), 0, 512, columns, table, grid, False)
-                return carry
-
-            lax.fori_loop(0, POINTS // 256, early, 0)
-
-    def part_of(ref, i):
-        return ref.at[:, pl.ds(pl.multiple_of(i * 256, 256), 256)]
-
-    def points(i, carry):
-        synthesise(i, slice(0, 768), 1024, 1536, columns, table, grid, True)
-        synthesise(i, slice(768, 1152), 512, 1536, columns, table, grid, True)
-        pltpu.make_async_copy(part_of(grid, i), part_of(out_hbm, i), out_sem).start()
-        return carry
-
-    lax.fori_loop(0, POINTS // 256, points, 0)
-    pltpu.make_async_copy(grid, out_hbm, out_sem).wait()
-    for phase in range(3):
-        wait_sent(phase, *back[phase])
+        if i:
+            each_part((None, early, middle, late)[i])
+    for rows, sem in ((upper, out_sem.at[0]), (lower, out_sem.at[1])):
+        pltpu.make_async_copy(grid.at[rows], out_hbm.at[rows], sem).wait()
+    for i in range(4):
+        wait_sent(*back[i])
 
 
 def step(*inputs):
@@ -576,7 +586,7 @@
         in_specs=[hbm, hbm, vmem, smem, smem, smem] + [vmem] * 4,
         out_specs=hbm,
         scratch_shapes=[pltpu.VMEM(s, d) for s, d in scratch]
-        + [dma((3,)), dma, dma, dma((6,)), dma((6,)), dma((6,))],
+        + [dma((3,)), dma, dma((2,)), dma((7,)), dma((7,)), dma((7,))],
         compiler_params=pltpu.CompilerParams(
             vmem_limit_bytes=67043328, collective_id=0, has_side_effects=True
         ),

time: 119 us -> 118 us (level)
    pallas_call x1, Pallas kernels: 113 us -> 112 us  [step(): pl.pallas_call(step_kernel, out_shape=jax.ShapeDtypeStruct((1152, POINTS)...]
where the time goes in v6:
time: 118 us
  Pallas kernels  112 us (95%)
  local copies, waits for them, and re-layouts  6.03 us (5%)
    pallas_call x1, Pallas kernels, step(): pl.pallas_call(step_kernel, out_shape=jax.ShapeDtypeStruct((1152, POINTS)...  112 us
    unnamed x1, local copies, waits for them, and re-layouts  6.03 us

profile of v6, /device:TPU:1, one launch (start us, length us, event | category | flops | bytes accessed | tf_op | source)
XLA Modules:
  0.0 117.5 jit_solution(2401248802685048712)
XLA Ops:
  0.0 111.5 %shard_map.91 = bf16[1152,2816]{1,0:T(8,128)(2,1)} custom-call(bf16[1152,2816]{1,0:T(8,128)(2,1)} %bitcast.5, bf16[3,769,1280]{2,1,0:T(8,128)(2,1)} %legendre_hbm.1, s32[384]{0:T(512)} %pair_m.1, s32[384]{0:T(512)} %pair_m.1, s32[32]{0:T(128)} %band_counts.1, f32[1280]{0:T(1024)} %gauss.1, f32[32,32]{1,0:T(8,128)} %vert_modes.1, f32[1,32]{1,0:T(1,128)} %bitcast.6, ...), custom_call_target="tpu_custom_call" | custom-call | tf_op jit(solution)/shard_map/pallas_call | solution.py:583
  111.5 6.0 %copy.11 = bf16[3,48,8,2816]{3,2,1,0:T(8,128)(2,1)} copy(bf16[3,48,8,2816]{3,2,1,0:T(8,128)(2,1)} %bitcast.4) | data formatting | bytes 12976128
